TPU v7x, 512 devices: a whole 4x4x16 slice. The times are simulated.
512 devices in a mesh: grp: 8 (over y, core), row: 64 (over z, x).
Axes of the slice: x: 4, y: 4, z: 16, core: 2. Of those that a mesh axis runs over, the one named last changes fastest.
Arguments:
- test_panel: bfloat16 [64, 1048576], P(None, ('grp', 'row')), may hold values from -6 to 6
- node_scale: float32 [1048576], P(('grp', 'row')), may hold values from 0.3 to 5.2
- diag_blocks: bfloat16 [64, 1048576], P(None, ('grp', 'row')), may hold values from -0.3125 to 0.3125
- off_blocks: bfloat16 [5, 64, 1048576], P(None, None, ('grp', 'row')), may hold values from -0.3125 to 0.3125
- block_columns: int32 [5, 16384], P(None, ('grp', 'row')), may hold values from 0 to 127, as said below
- send_lists: int32 [32768, 2], P(('grp', 'row')), may hold values from -1 to 31, as said below
Outputs:
- basis_panel: float32 [64, 1048576], P(None, ('grp', 'row'))
- r_factor: float32 [64, 64], replicated
Inputs may be any that keep to these rules, and one draw needn't show every extreme that they name: `send_lists`: row r of a device's list holds, in its first entries, distinct local block rows of that device whose panel blocks device r of the same group along row reads, and -1 in the rest. A row for a device at cycle distance at most 3 along row (wrapping within the group, the device itself included) holds 1 to 2 blocks; the row for the device itself always holds exactly 2, and one more near row may hold 2; a row for a farther device holds exactly one block. `block_columns`: entry (k, b) = s * 2 + j names entry j of the list that device s of the reader's group along row holds for the reader; that entry is never -1. Every live entry of the lists held for a device is named by some entry of that device's block rows.
All inputs are finite; a program needn't handle non-finite values.
Results may differ from a plain program's by a relative error of at most 0.003.
Values may be sent and summed in bfloat16 or wider, within the bound.
No kernel may reach another device: no remote copies, remote signals or barrier semaphores. Data moves between devices by JAX's collectives and lax.ppermute only.
A program may use at most 64 MiB of HBM per device.

v0:
```python
import math

import jax
import jax.numpy as jnp
from jax import lax
from jax.sharding import PartitionSpec as P


def partner_2(shard, axis, apart):
    return lax.ppermute(shard, axis, [(i, i ^ 1 << apart) for i in range(lax.axis_size(axis))])


def lower_factor(matrix):
    partial_gram_matrix = jnp.dot(matrix, matrix.T, precision=lax.Precision.HIGHEST)
    first_factor = jnp.linalg.cholesky(partial_gram_matrix)
    rotated = lax.linalg.triangular_solve(first_factor, matrix, left_side=True, lower=True)
    second = jnp.linalg.cholesky(jnp.dot(rotated, rotated.T, precision=lax.Precision.HIGHEST))
    return jnp.dot(first_factor, second, precision=lax.Precision.HIGHEST)


def merge_pair(first_factor, second_factor):
    return lower_factor(jnp.concatenate([first_factor, second_factor], axis=1))


def pack_rows(block_major, indices):
    is_valid = indices >= 0
    clipped = jnp.maximum(indices, 0)
    fetched = jnp.take(block_major, clipped, axis=0)
    return jnp.where(is_valid[..., None], fetched, jnp.zeros((), fetched.dtype))


def shards(test_panel, node_scale, diag_blocks, off_blocks, block_columns, send_lists):
    panel_width, local_nodes = test_panel.shape
    block_size = diag_blocks.shape[0]
    block_rows = local_nodes // block_size
    off_count = off_blocks.shape[0]
    row_count = lax.axis_size("row")
    capacity = send_lists.shape[1]
    node_count = local_nodes * lax.axis_size("grp") * row_count
    scaled = (test_panel.astype(jnp.float32) * node_scale[None, :]).astype(jnp.bfloat16)
    by_block = scaled.reshape(panel_width, block_rows, block_size)
    diag_part = jnp.einsum(
        "mik,kif->mif",
        by_block,
        diag_blocks.reshape(block_size, block_rows, block_size),
        preferred_element_type=jnp.float32,
    )
    block_major = by_block.transpose(1, 0, 2).reshape(block_rows, panel_width * block_size)
    my_rank = lax.axis_index("row")
    payload = pack_rows(block_major, send_lists)
    arrived = lax.all_to_all(payload, "row", split_axis=0, concat_axis=0, tiled=True)
    received = arrived.reshape(row_count * capacity, panel_width * block_size)
    fetched = jnp.take(received, block_columns, axis=0).reshape(
        off_count, block_rows, panel_width, block_size
    )
    off_part = jnp.einsum(
        "kbpc,kcbn->pbn",
        fetched,
        off_blocks.reshape(off_count, block_size, block_rows, block_size),
        preferred_element_type=jnp.float32,
    )
    sketch = (diag_part + off_part).reshape(panel_width, local_nodes) * node_scale[None, :]
    factor_low = lower_factor(sketch * (1.0 / math.sqrt(node_count)))
    for which_bit in range(row_count.bit_length() - 1):
        partner = partner_2(factor_low, "row", which_bit)
        lower_triangle_flag = my_rank // (1 << which_bit) % 2 == 0
        factor_low = merge_pair(
            jnp.where(lower_triangle_flag, factor_low, partner),
            jnp.where(lower_triangle_flag, partner, factor_low),
        )
    group_rank = lax.axis_index("grp")
    for which_bit in range(lax.axis_size("grp").bit_length() - 1):
        partner = partner_2(factor_low, "grp", which_bit)
        lower_triangle_flag = group_rank // (1 << which_bit) % 2 == 0
        factor_low = merge_pair(
            jnp.where(lower_triangle_flag, factor_low, partner),
            jnp.where(lower_triangle_flag, partner, factor_low),
        )
    basis_out = lax.linalg.triangular_solve(factor_low, sketch, left_side=True, lower=True)
    return (basis_out, factor_low.T)


def solution(mesh):
    in_specs = (
        P(None, ("grp", "row")),
        P(("grp", "row")),
        P(None, ("grp", "row")),
        P(None, None, ("grp", "row")),
        P(None, ("grp", "row")),
        P(("grp", "row"), None),
    )
    out_specs = (P(None, ("grp", "row")), P())
    return jax.shard_map(shards, mesh=mesh, in_specs=in_specs, out_specs=out_specs, check_vma=False)
```

profile of v0, /device:TPU:1, one launch (start us, length us, event | category | flops | bytes accessed | tf_op | source)
XLA Modules:
  0.0 380.7 jit_solution(5433530632760540996)
XLA Ops:
  9.0 19.1 %all-to-all-start = ((bf16[64,2,4096]{2,1,0:T(2,128)(2,1)}), bf16[64,2,4096]{2,1,0:T(2,128)(2,1)S(1)}, u32[]{:S(2)}, u32[]{:S(2)}) async-start(bf16[64,2,4096]{2,1,0:T(2,128)(2,1)} %broadcast_select_fusion.1), calls=%async_computation | async-start | bytes 2097152 | tf_op jit(solution)/shard_map/all_to_all | solution.py:51
  28.3 3.8 reshape.67
  33.6 45.9 %all-to-all-done = bf16[64,2,4096]{2,1,0:T(2,128)(2,1)S(1)} async-done(((bf16[64,2,4096]{2,1,0:T(2,128)(2,1)}), bf16[64,2,4096]{2,1,0:T(2,128)(2,1)S(1)}, u32[]{:S(2)}, u32[]{:S(2)}) %all-to-all-start) | async-done | bytes 1048608 | tf_op jit(solution)/shard_map/all_to_all | solution.py:51
  81.3 4.4 %gather.12 = bf16[5,32,64,64]{3,2,1,0:T(8,128)(2,1)} reshape(bf16[160,4096]{1,0:T(8,128)(2,1)S(1)} %gather_fusion.1) | data formatting | bytes 2621440 | tf_op jit(solution)/shard_map/jit(_take)/gather | solution.py:53
  85.7 4.9 %fusion.3 = f32[32,64,64]{2,1,0:T(8,128)S(1)} fusion(bf16[5,64,32,64]{3,2,1,0:T(8,128)(2,1)} %reshape.67, bf16[5,32,64,64]{3,2,1,0:T(8,128)(2,1)} %gather.12, pred[5,32]{0,1:T(8,128)(4,1)S(1)} %copy.40), kind=kOutput, calls=%fused_computation.8 | convolution fusion | flops 84541440 | bytes 3145888 | tf_op jit(solution)/shard_map/kbpc,kcbn->pbn/dot_general | solution.py:56
  92.8 5.8 %cholesky.314 = f32[64,64]{1,0:T(8,128)S(1)} custom-call(f32[64,64]{1,0:T(8,128)S(1)} %fusion.61), custom_call_target="Cholesky" | custom-call | tf_op jit(solution)/shard_map/jit(cholesky)/cholesky | solution.py:15
  99.9 4.9 %custom-call.17 = f32[1,64,64]{1,2,0:T(8,128)S(1)} custom-call(f32[1,64,64]{2,1,0:T(8,128)S(1)} %fusion.94), custom_call_target="InvertDiagBlocksLowerTriangular" | custom-call | tf_op jit(solution)/shard_map/triangular_solve/custom-call.0 | solution.py:16
  106.5 5.8 %cholesky.325 = f32[64,64]{1,0:T(8,128)S(1)} custom-call(f32[64,64]{1,0:T(8,128)S(1)} %fusion.59), custom_call_target="Cholesky" | custom-call | tf_op jit(solution)/shard_map/jit(cholesky)/cholesky | solution.py:17
  114.5 4.8 %collective-permute-start = (f32[64,64]{1,0:T(8,128)S(1)}, f32[64,64]{1,0:T(8,128)S(1)}, u32[]{:S(2)}, u32[]{:S(2)}) collective-permute-start(f32[64,64]{1,0:T(8,128)S(1)} %fusion.92), channel_id=1, source_target_pairs={{0,1},{1,0},{2,3},{3,2},{4,5},{5,4},{6,7},{7,6},{8,9},{9,8},{10,11... | collective-permute-start | bytes 49160 | tf_op jit(solution)/shard_map/ppermute | solution.py:10
  120.8 5.8 %cholesky.336 = f32[64,64]{1,0:T(8,128)S(1)} custom-call(f32[64,64]{1,0:T(8,128)S(1)} %fusion.58), custom_call_target="Cholesky" | custom-call | tf_op jit(solution)/shard_map/jit(cholesky)/cholesky | solution.py:15
  128.0 4.9 %custom-call.18 = f32[1,64,64]{1,2,0:T(8,128)S(1)} custom-call(f32[1,64,64]{2,1,0:T(8,128)S(1)} %fusion.97), custom_call_target="InvertDiagBlocksLowerTriangular" | custom-call | tf_op jit(solution)/shard_map/triangular_solve/custom-call.2 | solution.py:16
  133.5 5.8 %cholesky.347 = f32[64,64]{1,0:T(8,128)S(1)} custom-call(f32[64,64]{1,0:T(8,128)S(1)} %fusion.55), custom_call_target="Cholesky" | custom-call | tf_op jit(solution)/shard_map/jit(cholesky)/cholesky | solution.py:17
  141.5 5.8 %collective-permute-start.1 = (f32[64,64]{1,0:T(8,128)S(1)}, f32[64,64]{1,0:T(8,128)S(1)}, u32[]{:S(2)}, u32[]{:S(2)}) collective-permute-start(f32[64,64]{1,0:T(8,128)S(1)} %fusion.95), channel_id=1, source_target_pairs={{0,2},{1,3},{2,0},{3,1},{4,6},{5,7},{6,4},{7,5},{8,10},{9,11},{10,... | collective-permute-start | bytes 49160 | tf_op jit(solution)/shard_map/ppermute | solution.py:10
  148.9 5.8 %cholesky.358 = f32[64,64]{1,0:T(8,128)S(1)} custom-call(f32[64,64]{1,0:T(8,128)S(1)} %fusion.54), custom_call_target="Cholesky" | custom-call | tf_op jit(solution)/shard_map/jit(cholesky)/cholesky | solution.py:15
  156.1 4.9 %custom-call.19 = f32[1,64,64]{1,2,0:T(8,128)S(1)} custom-call(f32[1,64,64]{2,1,0:T(8,128)S(1)} %fusion.100), custom_call_target="InvertDiagBlocksLowerTriangular" | custom-call | tf_op jit(solution)/shard_map/triangular_solve/custom-call.2 | solution.py:16
  161.6 5.8 %cholesky.369 = f32[64,64]{1,0:T(8,128)S(1)} custom-call(f32[64,64]{1,0:T(8,128)S(1)} %fusion.51), custom_call_target="Cholesky" | custom-call | tf_op jit(solution)/shard_map/jit(cholesky)/cholesky | solution.py:17
  171.5 2.7 collective-permute-done.2
  174.6 5.8 %cholesky.380 = f32[64,64]{1,0:T(8,128)S(1)} custom-call(f32[64,64]{1,0:T(8,128)S(1)} %fusion.50), custom_call_target="Cholesky" | custom-call | tf_op jit(solution)/shard_map/jit(cholesky)/cholesky | solution.py:15
  181.8 4.9 %custom-call.20 = f32[1,64,64]{1,2,0:T(8,128)S(1)} custom-call(f32[1,64,64]{2,1,0:T(8,128)S(1)} %fusion.103), custom_call_target="InvertDiagBlocksLowerTriangular" | custom-call | tf_op jit(solution)/shard_map/triangular_solve/custom-call.2 | solution.py:16
  187.2 5.8 %cholesky.391 = f32[64,64]{1,0:T(8,128)S(1)} custom-call(f32[64,64]{1,0:T(8,128)S(1)} %fusion.47), custom_call_target="Cholesky" | custom-call | tf_op jit(solution)/shard_map/jit(cholesky)/cholesky | solution.py:17
  195.2 2.6 collective-permute-start.3
  197.8 3.0 collective-permute-done.3
  201.2 5.8 %cholesky.402 = f32[64,64]{1,0:T(8,128)S(1)} custom-call(f32[64,64]{1,0:T(8,128)S(1)} %fusion.46), custom_call_target="Cholesky" | custom-call | tf_op jit(solution)/shard_map/jit(cholesky)/cholesky | solution.py:15
  208.4 4.9 %custom-call.21 = f32[1,64,64]{1,2,0:T(8,128)S(1)} custom-call(f32[1,64,64]{2,1,0:T(8,128)S(1)} %fusion.106), custom_call_target="InvertDiagBlocksLowerTriangular" | custom-call | tf_op jit(solution)/shard_map/triangular_solve/custom-call.2 | solution.py:16
  213.9 5.8 %cholesky.413 = f32[64,64]{1,0:T(8,128)S(1)} custom-call(f32[64,64]{1,0:T(8,128)S(1)} %fusion.43), custom_call_target="Cholesky" | custom-call | tf_op jit(solution)/shard_map/jit(cholesky)/cholesky | solution.py:17
  221.9 2.5 collective-permute-start.4
  224.4 6.4 %collective-permute-done.4 = f32[64,64]{1,0:T(8,128)S(1)} collective-permute-done((f32[64,64]{1,0:T(8,128)S(1)}, f32[64,64]{1,0:T(8,128)S(1)}, u32[]{:S(2)}, u32[]{:S(2)}) %collective-permute-start.4) | collective-permute-done | bytes 16416 | tf_op jit(solution)/shard_map/ppermute | solution.py:10
  231.2 5.8 %cholesky.424 = f32[64,64]{1,0:T(8,128)S(1)} custom-call(f32[64,64]{1,0:T(8,128)S(1)} %fusion.42), custom_call_target="Cholesky" | custom-call | tf_op jit(solution)/shard_map/jit(cholesky)/cholesky | solution.py:15
  238.3 4.9 %custom-call.22 = f32[1,64,64]{1,2,0:T(8,128)S(1)} custom-call(f32[1,64,64]{2,1,0:T(8,128)S(1)} %fusion.109), custom_call_target="InvertDiagBlocksLowerTriangular" | custom-call | tf_op jit(solution)/shard_map/triangular_solve/custom-call.2 | solution.py:16
  243.8 5.8 %cholesky.435 = f32[64,64]{1,0:T(8,128)S(1)} custom-call(f32[64,64]{1,0:T(8,128)S(1)} %fusion.39), custom_call_target="Cholesky" | custom-call | tf_op jit(solution)/shard_map/jit(cholesky)/cholesky | solution.py:17
  251.8 4.0 %collective-permute-start.5 = (f32[64,64]{1,0:T(8,128)S(1)}, f32[64,64]{1,0:T(8,128)S(1)}, u32[]{:S(2)}, u32[]{:S(2)}) collective-permute-start(f32[64,64]{1,0:T(8,128)S(1)} %fusion.107), channel_id=1, source_target_pairs={{0,32},{1,33},{2,34},{3,35},{4,36},{5,37},{6,38},{7,39},{8,40},{9,... | collective-permute-start | bytes 49160 | tf_op jit(solution)/shard_map/ppermute | solution.py:10
  255.8 9.3 %collective-permute-done.5 = f32[64,64]{1,0:T(8,128)S(1)} collective-permute-done((f32[64,64]{1,0:T(8,128)S(1)}, f32[64,64]{1,0:T(8,128)S(1)}, u32[]{:S(2)}, u32[]{:S(2)}) %collective-permute-start.5) | collective-permute-done | bytes 16416 | tf_op jit(solution)/shard_map/ppermute | solution.py:10
  265.5 5.8 %cholesky.446 = f32[64,64]{1,0:T(8,128)S(1)} custom-call(f32[64,64]{1,0:T(8,128)S(1)} %fusion.38), custom_call_target="Cholesky" | custom-call | tf_op jit(solution)/shard_map/jit(cholesky)/cholesky | solution.py:15
  272.7 4.9 %custom-call.23 = f32[1,64,64]{1,2,0:T(8,128)S(1)} custom-call(f32[1,64,64]{2,1,0:T(8,128)S(1)} %fusion.112), custom_call_target="InvertDiagBlocksLowerTriangular" | custom-call | tf_op jit(solution)/shard_map/triangular_solve/custom-call.2 | solution.py:16
  278.2 5.8 %cholesky.457 = f32[64,64]{1,0:T(8,128)S(1)} custom-call(f32[64,64]{1,0:T(8,128)S(1)} %fusion.35), custom_call_target="Cholesky" | custom-call | tf_op jit(solution)/shard_map/jit(cholesky)/cholesky | solution.py:17
  286.2 12.6 %collective-permute-start.6 = (f32[64,64]{1,0:T(8,128)S(1)}, f32[64,64]{1,0:T(8,128)S(1)}, u32[]{:S(2)}, u32[]{:S(2)}) collective-permute-start(f32[64,64]{1,0:T(8,128)S(1)} %fusion.110), channel_id=1, source_target_pairs={{0,64},{64,0},{128,192},{192,128},{256,320},{320,256},{384,448},{4... | collective-permute-start | bytes 49160 | tf_op jit(solution)/shard_map/ppermute | solution.py:10
  299.7 5.8 %cholesky.468 = f32[64,64]{1,0:T(8,128)S(1)} custom-call(f32[64,64]{1,0:T(8,128)S(1)} %fusion.34), custom_call_target="Cholesky" | custom-call | tf_op jit(solution)/shard_map/jit(cholesky)/cholesky | solution.py:15
  306.9 4.9 %custom-call.24 = f32[1,64,64]{1,2,0:T(8,128)S(1)} custom-call(f32[1,64,64]{2,1,0:T(8,128)S(1)} %fusion.115), custom_call_target="InvertDiagBlocksLowerTriangular" | custom-call | tf_op jit(solution)/shard_map/triangular_solve/custom-call.2 | solution.py:16
  312.4 5.8 %cholesky.479 = f32[64,64]{1,0:T(8,128)S(1)} custom-call(f32[64,64]{1,0:T(8,128)S(1)} %fusion.31), custom_call_target="Cholesky" | custom-call | tf_op jit(solution)/shard_map/jit(cholesky)/cholesky | solution.py:17
  320.4 3.2 collective-permute-start.7
  325.4 5.8 %cholesky.490 = f32[64,64]{1,0:T(8,128)S(1)} custom-call(f32[64,64]{1,0:T(8,128)S(1)} %fusion.30), custom_call_target="Cholesky" | custom-call | tf_op jit(solution)/shard_map/jit(cholesky)/cholesky | solution.py:15
  332.6 4.9 %custom-call.25 = f32[1,64,64]{1,2,0:T(8,128)S(1)} custom-call(f32[1,64,64]{2,1,0:T(8,128)S(1)} %fusion.118), custom_call_target="InvertDiagBlocksLowerTriangular" | custom-call | tf_op jit(solution)/shard_map/triangular_solve/custom-call.2 | solution.py:16
  338.0 5.8 %cholesky.501 = f32[64,64]{1,0:T(8,128)S(1)} custom-call(f32[64,64]{1,0:T(8,128)S(1)} %fusion.27), custom_call_target="Cholesky" | custom-call | tf_op jit(solution)/shard_map/jit(cholesky)/cholesky | solution.py:17
  346.0 4.8 %collective-permute-start.8 = (f32[64,64]{1,0:T(8,128)S(1)}, f32[64,64]{1,0:T(8,128)S(1)}, u32[]{:S(2)}, u32[]{:S(2)}) collective-permute-start(f32[64,64]{1,0:T(8,128)S(1)} %fusion.116), channel_id=1, source_target_pairs={{0,256},{64,320},{128,384},{192,448},{256,0},{320,64},{384,128},{4... | collective-permute-start | bytes 49160 | tf_op jit(solution)/shard_map/ppermute | solution.py:10
  352.6 5.8 %cholesky.512 = f32[64,64]{1,0:T(8,128)S(1)} custom-call(f32[64,64]{1,0:T(8,128)S(1)} %fusion.26), custom_call_target="Cholesky" | custom-call | tf_op jit(solution)/shard_map/jit(cholesky)/cholesky | solution.py:15
  359.7 4.9 %custom-call.26 = f32[1,64,64]{1,2,0:T(8,128)S(1)} custom-call(f32[1,64,64]{2,1,0:T(8,128)S(1)} %fusion.121), custom_call_target="InvertDiagBlocksLowerTriangular" | custom-call | tf_op jit(solution)/shard_map/triangular_solve/custom-call.2 | solution.py:16
  365.2 5.8 %cholesky.523 = f32[64,64]{1,0:T(8,128)S(1)} custom-call(f32[64,64]{1,0:T(8,128)S(1)} %fusion.23), custom_call_target="Cholesky" | custom-call | tf_op jit(solution)/shard_map/jit(cholesky)/cholesky | solution.py:17
  373.2 4.9 %custom-call.27 = f32[1,64,64]{1,2,0:T(8,128)S(1)} custom-call(f32[1,64,64]{2,1,0:T(8,128)S(1)} %select_bitcast_fusion), custom_call_target="InvertDiagBlocksLowerTriangular" | custom-call | tf_op jit(solution)/shard_map/triangular_solve/custom-call.0 | solution.py:79
  (180 shorter events, 67.9 us)
Async XLA Ops:
  6.4 21.7 %copy-start.1 = (f32[2048]{0:T(1024)S(1)}, f32[2048]{0:T(1024)}, u32[]{:S(2)}) copy-start(f32[2048]{0:T(1024)} %param.12) | copy-start | bytes 24580
  6.4 21.8 %copy-start.2 = (s32[5,32]{1,0:T(8,128)S(1)}, s32[5,32]{1,0:T(8,128)}, u32[]{:S(2)}) copy-start(s32[5,32]{1,0:T(8,128)} %param.15) | copy-start | bytes 1924
  6.4 21.9 %copy-start = (bf16[5,64,2048]{2,1,0:T(8,128)(2,1)S(1)}, bf16[5,64,2048]{2,1,0:T(8,128)(2,1)}, u32[]{:S(2)}) copy-start(bf16[5,64,2048]{2,1,0:T(8,128)(2,1)} %param.14) | copy-start | bytes 3932164
  9.0 70.6 %all-to-all-start = ((bf16[64,2,4096]{2,1,0:T(2,128)(2,1)}), bf16[64,2,4096]{2,1,0:T(2,128)(2,1)S(1)}, u32[]{:S(2)}, u32[]{:S(2)}) async-start(bf16[64,2,4096]{2,1,0:T(2,128)(2,1)} %broadcast_select_fusion.1), calls=%async_computation | async-start | bytes 2097152 | tf_op jit(solution)/shard_map/all_to_all | solution.py:51
  114.5 6.0 %collective-permute-start = (f32[64,64]{1,0:T(8,128)S(1)}, f32[64,64]{1,0:T(8,128)S(1)}, u32[]{:S(2)}, u32[]{:S(2)}) collective-permute-start(f32[64,64]{1,0:T(8,128)S(1)} %fusion.92), channel_id=1, source_target_pairs={{0,1},{1,0},{2,3},{3,2},{4,5},{5,4},{6,7},{7,6},{8,9},{9,8},{10,11... | collective-permute-start | bytes 49160 | tf_op jit(solution)/shard_map/ppermute | solution.py:10
  141.5 7.1 %collective-permute-start.1 = (f32[64,64]{1,0:T(8,128)S(1)}, f32[64,64]{1,0:T(8,128)S(1)}, u32[]{:S(2)}, u32[]{:S(2)}) collective-permute-start(f32[64,64]{1,0:T(8,128)S(1)} %fusion.95), channel_id=1, source_target_pairs={{0,2},{1,3},{2,0},{3,1},{4,6},{5,7},{6,4},{7,5},{8,10},{9,11},{10,... | collective-permute-start | bytes 49160 | tf_op jit(solution)/shard_map/ppermute | solution.py:10
  169.5 4.7 %collective-permute-start.2 = (f32[64,64]{1,0:T(8,128)S(1)}, f32[64,64]{1,0:T(8,128)S(1)}, u32[]{:S(2)}, u32[]{:S(2)}) collective-permute-start(f32[64,64]{1,0:T(8,128)S(1)} %fusion.98), channel_id=1, source_target_pairs={{0,4},{1,5},{2,6},{3,7},{4,0},{5,1},{6,2},{7,3},{8,12},{9,13},{10,... | collective-permute-start | bytes 49160 | tf_op jit(solution)/shard_map/ppermute | solution.py:10
  195.2 5.6 %collective-permute-start.3 = (f32[64,64]{1,0:T(8,128)S(1)}, f32[64,64]{1,0:T(8,128)S(1)}, u32[]{:S(2)}, u32[]{:S(2)}) collective-permute-start(f32[64,64]{1,0:T(8,128)S(1)} %fusion.101), channel_id=1, source_target_pairs={{0,8},{1,9},{2,10},{3,11},{4,12},{5,13},{6,14},{7,15},{8,0},{9,1},... | collective-permute-start | bytes 49160 | tf_op jit(solution)/shard_map/ppermute | solution.py:10
  221.9 8.9 %collective-permute-start.4 = (f32[64,64]{1,0:T(8,128)S(1)}, f32[64,64]{1,0:T(8,128)S(1)}, u32[]{:S(2)}, u32[]{:S(2)}) collective-permute-start(f32[64,64]{1,0:T(8,128)S(1)} %fusion.104), channel_id=1, source_target_pairs={{0,16},{1,17},{2,18},{3,19},{4,20},{5,21},{6,22},{7,23},{8,24},{9,... | collective-permute-start | bytes 49160 | tf_op jit(solution)/shard_map/ppermute | solution.py:10
  251.8 13.4 %collective-permute-start.5 = (f32[64,64]{1,0:T(8,128)S(1)}, f32[64,64]{1,0:T(8,128)S(1)}, u32[]{:S(2)}, u32[]{:S(2)}) collective-permute-start(f32[64,64]{1,0:T(8,128)S(1)} %fusion.107), channel_id=1, source_target_pairs={{0,32},{1,33},{2,34},{3,35},{4,36},{5,37},{6,38},{7,39},{8,40},{9,... | collective-permute-start | bytes 49160 | tf_op jit(solution)/shard_map/ppermute | solution.py:10
  286.2 13.2 %collective-permute-start.6 = (f32[64,64]{1,0:T(8,128)S(1)}, f32[64,64]{1,0:T(8,128)S(1)}, u32[]{:S(2)}, u32[]{:S(2)}) collective-permute-start(f32[64,64]{1,0:T(8,128)S(1)} %fusion.110), channel_id=1, source_target_pairs={{0,64},{64,0},{128,192},{192,128},{256,320},{320,256},{384,448},{4... | collective-permute-start | bytes 49160 | tf_op jit(solution)/shard_map/ppermute | solution.py:10
  320.4 4.7 %collective-permute-start.7 = (f32[64,64]{1,0:T(8,128)S(1)}, f32[64,64]{1,0:T(8,128)S(1)}, u32[]{:S(2)}, u32[]{:S(2)}) collective-permute-start(f32[64,64]{1,0:T(8,128)S(1)} %fusion.113), channel_id=1, source_target_pairs={{0,128},{64,192},{128,0},{192,64},{256,384},{320,448},{384,256},{4... | collective-permute-start | bytes 49160 | tf_op jit(solution)/shard_map/ppermute | solution.py:10
  346.0 6.2 %collective-permute-start.8 = (f32[64,64]{1,0:T(8,128)S(1)}, f32[64,64]{1,0:T(8,128)S(1)}, u32[]{:S(2)}, u32[]{:S(2)}) collective-permute-start(f32[64,64]{1,0:T(8,128)S(1)} %fusion.116), channel_id=1, source_target_pairs={{0,256},{64,320},{128,384},{192,448},{256,0},{320,64},{384,128},{4... | collective-permute-start | bytes 49160 | tf_op jit(solution)/shard_map/ppermute | solution.py:10
where the time goes:
time: 388 us; the launch traced here: 381 us
  other arithmetic  196 us (51%)
  waiting for transfers between devices  73 us (19%)
  starting transfers between devices  61.3 us (16%)
  matrix products  29.9 us (8%)
  local copies, waits for them, and re-layouts  18.4 us (5%)
    another operation x30, other arithmetic, lower_factor(): jnp.linalg.cholesky(jnp.dot(rotated, rotated.T, precision=lax.Precision.H...  65.2 us
    another operation x30, other arithmetic, lower_factor(): first_factor = jnp.linalg.cholesky(partial_gram_matrix)  65.2 us
    another operation x20, other arithmetic, lower_factor(): lax.linalg.triangular_solve(first_factor, matrix, left_side=True, lower=T...  55.5 us
    all_to_all x1, waiting for transfers between devices, shards(): lax.all_to_all(payload, 'row', split_axis=0, concat_axis=0, tiled=True)  45.9 us
    ppermute x9, starting transfers between devices, partner_2(): lax.ppermute(shard, axis, [(i, i ^ 1 << apart) for i in range(lax.axis_si...  42.2 us
    ppermute x9, waiting for transfers between devices, partner_2(): lax.ppermute(shard, axis, [(i, i ^ 1 << apart) for i in range(lax.axis_si...  27.1 us
    all_to_all x1, starting transfers between devices, shards(): lax.all_to_all(payload, 'row', split_axis=0, concat_axis=0, tiled=True)  19.1 us
    dot_general x10, matrix products, lower_factor(): return jnp.dot(first_factor, second, precision=lax.Precision.HIGHEST)  14.5 us
  transfers between devices with their start and end apart: 10, of which 10 were waited for; matrix products, arithmetic and copies ran while one was open for 1% of the time, Pallas kernels for 0%

commit v1 on v0

v1 whole, which is shorter than its diff:
```python
import jax
import jax.numpy as jnp
from jax import lax
from jax.experimental import pallas as pl
from jax.experimental.pallas import tpu as pltpu
from jax.sharding import Mesh, PartitionSpec as P

NY, NC, NZ, NX = 4, 2, 16, 4
PLANE = ("y", "c", "x")
NPLANE = NY * NC * NX
MIB = 1 << 20


def vmem():
    return pl.BlockSpec(memory_space=pltpu.VMEM)


def smem():
    return pl.BlockSpec(memory_space=pltpu.SMEM)


def left_half(rows):
    return lax.broadcasted_iota(jnp.int32, (rows, 128), 1) < 64


def pack_kernel(lists, panel, scale, scaled, payload, blocks):
    left = left_half(32)
    for i in range(panel.shape[1] // 128):
        cols = slice(128 * i, 128 * i + 128)
        slab = panel[:, cols].astype(jnp.float32) * scale[i : i + 1, :]
        scaled[:, cols] = slab.astype(jnp.bfloat16)
        top, low = slab[:32], slab[32:]
        even = jnp.where(left, top, pltpu.roll(low, 64, 1))
        odd = jnp.where(left, pltpu.roll(top, 64, 1), low)
        blocks[2 * i] = even.astype(jnp.bfloat16)
        blocks[2 * i + 1] = odd.astype(jnp.bfloat16)
    z, x = lax.axis_index("z"), lax.axis_index("x")
    rank = z * NX + x
    for to in range(NX):
        for zz in range(NZ):
            payload[to, zz] = blocks[jnp.maximum(lists[zz * NX + to, 0], 0)]
        step = lax.rem(to - x + NX, NX)
        first = lax.rem(rank + step, NZ * NX)
        second = lax.rem(rank + step - NX + NZ * NX, NZ * NX)
        payload[to, NZ] = blocks[jnp.maximum(lists[first, 1], 0)]
        payload[to, NZ + 1] = blocks[jnp.maximum(lists[second, 1], 0)]


def multiply_kernel(where_at, main, near, above, below, scaled, scale, diag, off, halves, gram, table):
    left = left_half(32)

    def spread(at, packed):
        wide = packed.astype(jnp.float32)
        turned = pltpu.roll(wide, 64, 1)
        table[at, :32] = jnp.where(left, wide, turned).astype(jnp.bfloat16)
        table[at, 32:] = jnp.where(left, turned, wide).astype(jnp.bfloat16)

    for s in range(NZ * NX):
        spread(s, main[s // NX, s % NX])
    for s in range(NX):
        spread(64 + s, near[s, 0])
        spread(68 + s, near[s, 1])
        spread(72 + s, above[s])
        spread(76 + s, below[s])

    left64 = left_half(64)
    same = (lax.broadcasted_iota(jnp.int32, (128, 128), 0) < 64) == left_half(128)
    zero = jnp.zeros((), jnp.bfloat16)
    total = jnp.zeros((128, 128), jnp.float32)
    for i in range(scaled.shape[1] // 128):
        cols = slice(128 * i, 128 * i + 128)
        own = diag[:, cols]
        own = jnp.where(same, jnp.concatenate([own, own], axis=0), zero)
        product = jnp.dot(scaled[:, cols], own, preferred_element_type=jnp.float32)
        rows = []
        for b in (2 * i, 2 * i + 1):
            read = [table[where_at[k, b]] for k in range(5)]
            first = jnp.where(left64, read[0], read[1])
            second = jnp.where(left64, read[2], read[3])
            third = jnp.where(left64, read[4], zero)
            rows.append(jnp.concatenate([first, second, third], axis=1))
        weights = [off[k, :, cols] for k in range(5)]
        weights.append(jnp.zeros((64, 128), jnp.bfloat16))
        both = jnp.dot(
            jnp.concatenate(rows, axis=0),
            jnp.concatenate(weights, axis=0),
            preferred_element_type=jnp.float32,
        )
        product = product + jnp.where(left64, both[:64], both[64:])
        sketch = product * scale[i : i + 1, :]
        high = sketch.astype(jnp.bfloat16)
        low = (sketch - high.astype(jnp.float32)).astype(jnp.bfloat16)
        pair = jnp.concatenate([high, low], axis=0)
        halves[:, cols] = pair
        total = total + lax.dot_general(
            pair, pair, (((1,), (1,)), ((), ())), preferred_element_type=jnp.float32
        )
    total = total[:64] + total[64:]
    total = total + pltpu.roll(total, 64, 1)
    gram[:, 0, :] = jnp.where(left, total[:32], total[32:])


def finish_kernel(node_count, gram, halves, basis, factor):
    packed = gram[:, 0, :] * (1.0 / node_count)
    turned = pltpu.roll(packed, 64, 1)
    full = jnp.concatenate([packed, turned], axis=0)
    lane = lax.broadcasted_iota(jnp.int32, (64, 128), 1)
    row = lax.broadcasted_iota(jnp.int32, (64, 128), 0)
    work = jnp.where(lane < 64, full, (lane - 64 == row).astype(jnp.float32))
    for k in range(64):
        column = jnp.broadcast_to(work[:, k : k + 1], (64, 128))
        pivot = column[k : k + 1, :]
        inverse = lax.rsqrt(pivot)
        inverse = inverse * (1.5 - 0.5 * pivot * inverse * inverse)
        scaled_row = work[k : k + 1, :] * inverse
        factor_column = column * inverse
        work = jnp.where(
            row > k, work - factor_column * scaled_row, jnp.where(row == k, scaled_row, work)
        )
    factor[...] = jnp.where(row <= lane, work, 0.0)[:, :64]
    solve = pltpu.roll(work, 64, 1)
    solve = jnp.where((lane < 64) & (lane <= row), solve, 0.0)
    high = solve.astype(jnp.bfloat16)
    low = (solve - high.astype(jnp.float32)).astype(jnp.bfloat16)
    twice = jnp.where(lane < 64, solve, pltpu.roll(solve, 64, 1)).astype(jnp.bfloat16)
    left = jnp.concatenate([twice, low], axis=0)
    for i in range(halves.shape[1] // 256):
        cols = slice(256 * i, 256 * i + 256)
        both = jnp.dot(left, halves[:, cols], preferred_element_type=jnp.float32)
        basis[:, cols] = both[:64] + both[64:]


def shards(test_panel, node_scale, diag_blocks, off_blocks, block_columns, send_lists):
    panel_width, local_nodes = test_panel.shape
    node_count = local_nodes * NY * NC * NZ * NX
    scale = node_scale.reshape(local_nodes // 128, 128)
    scaled, payload = pl.pallas_call(
        pack_kernel,
        out_shape=(
            jax.ShapeDtypeStruct((64, local_nodes), jnp.bfloat16),
            jax.ShapeDtypeStruct((NX, NZ + 2, 32, 128), jnp.bfloat16),
        ),
        in_specs=[smem(), vmem(), vmem()],
        out_specs=(vmem(), vmem()),
        scratch_shapes=[pltpu.VMEM((32, 32, 128), jnp.bfloat16)],
        compiler_params=pltpu.CompilerParams(vmem_limit_bytes=8 * MIB),
        name="pack",
    )(send_lists, test_panel, scale)

    z, x = lax.axis_index("z"), lax.axis_index("x")
    source, entry = block_columns // 2, block_columns % 2
    source_z, source_x = source // NX, source % NX
    same = 64 + jnp.where(source_x <= x, source_x, NX + source_x)
    other = jnp.where(source_z == (z + NZ - 1) % NZ, 72, 76) + source_x
    where_at = jnp.where(entry == 0, source, jnp.where(source_z == z, same, other))

    near = lax.all_to_all(payload, "x", 0, 0, tiled=True)
    up = [(i, (i + 1) % NZ) for i in range(NZ)]
    down = [((i + 1) % NZ, i) for i in range(NZ)]
    above = lax.ppermute(near[:, NZ], "z", up)
    below = lax.ppermute(near[:, NZ + 1], "z", down)
    main = lax.all_to_all(near[:, :NZ].transpose(1, 0, 2, 3), "z", 0, 0, tiled=True)

    halves, gram = pl.pallas_call(
        multiply_kernel,
        out_shape=(
            jax.ShapeDtypeStruct((128, local_nodes), jnp.bfloat16),
            jax.ShapeDtypeStruct((32, 1, 128), jnp.float32),
        ),
        in_specs=[smem()] + [vmem()] * 8,
        out_specs=(vmem(), vmem()),
        scratch_shapes=[pltpu.VMEM((80, 64, 128), jnp.bfloat16)],
        compiler_params=pltpu.CompilerParams(vmem_limit_bytes=16 * MIB),
        name="multiply",
    )(where_at, main, near[:, NZ:], above, below, scaled, scale, diag_blocks, off_blocks)

    part = lax.all_to_all(gram, PLANE, 0, 0, tiled=True).sum(0)
    part = lax.all_to_all(jnp.broadcast_to(part[None], (NZ, 1, 128)), "z", 0, 0, tiled=True).sum(0)
    gram = lax.all_to_all(jnp.broadcast_to(part[None], (NPLANE, 1, 128)), PLANE, 0, 0, tiled=True)

    def finish(*refs):
        finish_kernel(node_count, *refs)

    return pl.pallas_call(
        finish,
        out_shape=(
            jax.ShapeDtypeStruct((64, local_nodes), jnp.float32),
            jax.ShapeDtypeStruct((64, 64), jnp.float32),
        ),
        in_specs=[vmem(), vmem()],
        out_specs=(vmem(), vmem()),
        compiler_params=pltpu.CompilerParams(vmem_limit_bytes=8 * MIB),
        name="finish",
    )(gram, halves)


def solution(mesh):
    split = Mesh(mesh.devices.reshape(NY, NC, NZ, NX), ("y", "c", "z", "x"))
    every = ("y", "c", "z", "x")
    in_specs = (
        P(None, every),
        P(every),
        P(None, every),
        P(None, None, every),
        P(None, every),
        P(every, None),
    )
    out_specs = (P(None, every), P())
    return jax.shard_map(shards, mesh=split, in_specs=in_specs, out_specs=out_specs, check_vma=False)
```

time: 388 us -> 117 us (0.30); the launches traced: 381 us -> 117 us
  other arithmetic: 196 us -> 0.09 us
  blocking collectives: 0 us -> 61.9 us
  waiting for transfers between devices: 73 us -> 14.6 us
  starting transfers between devices: 61.3 us -> 23.1 us
  matrix products: 29.9 us -> 0 us
  local copies, waits for them, and re-layouts: 18.4 us -> 4.17 us
  Pallas kernels: 0 us -> 11.9 us
    another operation x82 -> x0, other arithmetic: 191 us -> none  [the longest x30 65.2 us: lower_factor(): jnp.linalg.cholesky(jnp.dot(rotated, rotated.T, precision=lax.Precision.H...]
    all_to_all x0 -> x4, blocking collectives: none -> 61.9 us  [the longest x1 20.4 us: shards(): part = lax.all_to_all(gram, PLANE, 0, 0, tiled=True).sum(0)]
    all_to_all x1, waiting for transfers between devices: 45.9 us -> 0.01 us  [shards(): lax.all_to_all(near[:, :NZ].transpose(1, 0, 2, 3), 'z', 0, 0, tiled=True)]
    ppermute x9 -> x2, starting transfers between devices: 42.2 us -> 6.39 us  [the longest x1 4.47 us: shards(): below = lax.ppermute(near[:, NZ + 1], 'z', down)]
    dot_general x32 -> x0, matrix products: 25.4 us -> none  [the longest x10 14.5 us: lower_factor(): return jnp.dot(first_factor, second, precision=lax.Precision.HIGHEST)]
    ppermute x9 -> x2, waiting for transfers between devices: 27.1 us -> 14.6 us  [the longest x1 14.6 us: shards(): below = lax.ppermute(near[:, NZ + 1], 'z', down)]
    pallas_call x0 -> x3, Pallas kernels: none -> 11.9 us  [the longest x1 6.91 us: shards(): pl.pallas_call(finish, out_shape=(jax.ShapeDtypeStruct((64, local_nodes),...]
    gather x4 -> x0, local copies, waits for them, and re-layouts: 7.62 us -> none  [the longest x2 5.72 us: shards(): jnp.take(received, block_columns, axis=0)]
  transfers between devices with their start and end apart: 10 -> 3, of which waited for: 10 -> 1; matrix products, arithmetic and copies ran while one was open for 1% -> 1% of each run, Pallas kernels for 0% -> 0%
where the time goes in v1:
time: 117 us
  blocking collectives  61.9 us (53%)
  starting transfers between devices  23.1 us (20%)
  waiting for transfers between devices  14.6 us (12%)
  Pallas kernels  11.9 us (10%)
  local copies, waits for them, and re-layouts  4.17 us (4%)
    all_to_all x1, blocking collectives, shards(): part = lax.all_to_all(gram, PLANE, 0, 0, tiled=True).sum(0)  20.4 us
    all_to_all x1, blocking collectives, shards(): lax.all_to_all(jnp.broadcast_to(part[None], (NZ, 1, 128)), 'z', 0, 0, til...  17.5 us
    all_to_all x1, starting transfers between devices, shards(): lax.all_to_all(near[:, :NZ].transpose(1, 0, 2, 3), 'z', 0, 0, tiled=True)  16.7 us
    ppermute x1, waiting for transfers between devices, shards(): below = lax.ppermute(near[:, NZ + 1], 'z', down)  14.6 us
    all_to_all x1, blocking collectives, shards(): lax.all_to_all(jnp.broadcast_to(part[None], (NPLANE, 1, 128)), PLANE, 0,...  12.1 us
    all_to_all x1, blocking collectives, shards(): near = lax.all_to_all(payload, 'x', 0, 0, tiled=True)  11.9 us
    pallas_call x1, Pallas kernels, shards(): pl.pallas_call(finish, out_shape=(jax.ShapeDtypeStruct((64, local_nodes),...  6.91 us
    ppermute x1, starting transfers between devices, shards(): below = lax.ppermute(near[:, NZ + 1], 'z', down)  4.47 us
  transfers between devices with their start and end apart: 3, of which 1 were waited for; matrix products, arithmetic and copies ran while one was open for 1% of the time, Pallas kernels for 0%

profile of v1, /device:TPU:1, one launch (start us, length us, event | category | flops | bytes accessed | tf_op | source)
XLA Modules:
  0.0 116.5 jit_solution(5319786090400860888)
XLA Ops:
  0.6 0.8 copy.19.lists
  1.4 0.0 copy-start.2
  1.4 0.9 copy-done.2
  2.3 0.0 copy-start.3
  2.4 0.7 copy-done.3
  3.0 1.3 %pack.1 = (bf16[64,2048]{1,0:T(8,128)(2,1)S(1)}, bf16[4,18,32,128]{3,2,1,0:T(8,128)(2,1)S(1)}) custom-call(s32[64,2]{1,0:T(8,128)S(1)} %copy.19.lists, bf16[64,2048]{1,0:T(8,128)(2,1)S(1)} %copy-done.2, f32[16,128]{1,0:T(8,128)S(1)} %bitcast.12), custom_call_target="tpu_custom_call" | custom-call | tf_op jit(solution)/shard_map/pack/pallas_call | solution.py:137
  4.3 11.9 %all_to_all.25 = bf16[4,18,32,128]{3,2,1,0:T(8,128)(2,1)S(1)} all-to-all(bf16[4,18,32,128]{3,2,1,0:T(8,128)(2,1)S(1)} %get-tuple-element.6), channel_id=1, replica_groups=mesh['y'=4,'c'=2,'z'=16,'x'=4] {'x'}, dimensions={0} | all-to-all | bytes 1179648 | tf_op jit(solution)/shard_map/all_to_all | solution.py:157
  16.3 0.0 copy-start.5
  16.3 0.0 copy-start.6
  16.3 0.0 copy-start
  16.3 0.0 copy-start.1
  16.3 0.0 copy-start.4
  16.3 0.9 copy_bitcast_fusion
  17.2 16.7 %all-to-all-start.1 = ((bf16[16,4,32,128]{3,2,1,0:T(8,128)(2,1)}), bf16[16,4,32,128]{3,2,1,0:T(8,128)(2,1)S(1)}, u32[]{:S(2)}, u32[]{:S(2)}) async-start(bf16[16,4,32,128]{3,2,1,0:T(8,128)(2,1)} %copy_bitcast_fusion), calls=%async_computation.1 | async-start | bytes 1048576 | tf_op jit(solution)/shard_map/all_to_all | solution.py:162
  33.9 0.0 copy-done.5
  33.9 4.5 %collective-permute-start.1 = (bf16[4,32,128]{2,1,0:T(8,128)(2,1)S(1)}, bf16[4,32,128]{2,1,0:T(8,128)(2,1)S(1)}, u32[]{:S(2)}, u32[]{:S(2)}) collective-permute-start(bf16[4,32,128]{2,1,0:T(8,128)(2,1)S(1)} %get-tuple-element.10), channel_id=1, source_target_pairs={{4,0},{8,4},{12,8},{16,12},{20,16},{24,20},{28,24},{32,28},{36,32}... | collective-permute-start | bytes 98312 | tf_op jit(solution)/shard_map/ppermute | solution.py:161
  38.4 1.9 %collective-permute-start = (bf16[4,32,128]{2,1,0:T(8,128)(2,1)S(1)}, bf16[4,32,128]{2,1,0:T(8,128)(2,1)S(1)}, u32[]{:S(2)}, u32[]{:S(2)}) collective-permute-start(bf16[4,32,128]{2,1,0:T(8,128)(2,1)S(1)} %get-tuple-element.11), channel_id=1, source_target_pairs={{0,4},{4,8},{8,12},{12,16},{16,20},{20,24},{24,28},{28,32},{32,36}... | collective-permute-start | bytes 98312 | tf_op jit(solution)/shard_map/ppermute | solution.py:160
  40.3 0.0 copy-done.6
  40.4 0.9 slice.17.near
  41.2 14.6 %collective-permute-done.1.below = bf16[4,32,128]{2,1,0:T(8,128)(2,1)S(1)} collective-permute-done((bf16[4,32,128]{2,1,0:T(8,128)(2,1)S(1)}, bf16[4,32,128]{2,1,0:T(8,128)(2,1)S(1)}, u32[]{:S(2)}, u32[]{:S(2)}) %collective-permute-start.1) | collective-permute-done | bytes 32800 | tf_op jit(solution)/shard_map/ppermute | solution.py:161
  55.9 0.0 collective-permute-done.above
  55.9 0.0 all-to-all-done.1.main
  55.9 0.0 copy-done
  55.9 0.0 copy-done.1
  55.9 0.0 copy-done.4
  55.9 3.7 %multiply.1 = (bf16[128,2048]{1,0:T(8,128)(2,1)S(1)}, f32[32,1,128]{2,1,0:T(1,128)S(1)}) custom-call(s32[5,32]{1,0:T(8,128)S(1)} %fusion.3.where_at, bf16[16,4,32,128]{3,2,1,0:T(8,128)(2,1)S(1)} %all-to-all-done.1.main, bf16[4,2,32,128]{3,2,1,0:T(8,128)(2,1)S(1)} %slice.17.near, bf16[4,32,128]{2,1,0:T(8,128)(2,1)S(1)} %collective-permute-done.above, ...), custom_call_target="tpu_custom_call" | custom-call | tf_op jit(solution)/shard_map/multiply/pallas_call | solution.py:164
  59.6 20.4 %all_to_all.26 = f32[32,1,128]{2,1,0:T(1,128)S(1)} all-to-all(f32[32,1,128]{2,1,0:T(1,128)S(1)} %get-tuple-element.8), channel_id=1, replica_groups=mesh['y'=4,'c'=2,'z'=16,'x'=4] {'y','c','x'}, dimensions={0} | all-to-all | bytes 32768 | tf_op jit(solution)/shard_map/all_to_all | solution.py:177
  79.9 0.1 reduce_sum.18
  80.0 17.5 %all_to_all.27 = f32[16,1,128]{2,1,0:T(1,128)S(1)} all-to-all(f32[16,1,128]{2,1,0:T(1,128)S(1)} %broadcast_in_dim.22), channel_id=1, replica_groups=mesh['y'=4,'c'=2,'z'=16,'x'=4] {'z'}, dimensions={0} | all-to-all | bytes 16384 | tf_op jit(solution)/shard_map/all_to_all | solution.py:178
  97.5 12.1 %all_to_all.28.refs_0_ = f32[32,1,128]{2,1,0:T(1,128)S(1)} all-to-all(f32[32,1,128]{2,1,0:T(1,128)S(1)} %broadcast_in_dim.23), channel_id=1, replica_groups=mesh['y'=4,'c'=2,'z'=16,'x'=4] {'y','c','x'}, dimensions={0} | all-to-all | bytes 32768 | tf_op jit(solution)/shard_map/all_to_all | solution.py:179
  109.6 6.9 %finish.1 = (f32[64,2048]{1,0:T(8,128)}, f32[64,64]{1,0:T(8,128)}) custom-call(f32[32,1,128]{2,1,0:T(1,128)S(1)} %all_to_all.28.refs_0_, bf16[128,2048]{1,0:T(8,128)(2,1)S(1)} %get-tuple-element.9.refs_1_), custom_call_target="tpu_custom_call" | custom-call | tf_op jit(solution)/shard_map/finish/pallas_call | solution.py:184
  (5 shorter events, 0.1 us)
Async XLA Ops:
  1.4 0.9 copy-start.2
  2.3 0.7 copy-start.3
  16.3 17.6 %copy-start.5 = (bf16[4,18,32,128]{3,2,1,0:T(8,128)(2,1)}, bf16[4,18,32,128]{3,2,1,0:T(8,128)(2,1)S(1)}, u32[]{:S(2)}) copy-start(bf16[4,18,32,128]{3,2,1,0:T(8,128)(2,1)S(1)} %all_to_all.25) | copy-start | bytes 1769476
  16.3 24.1 %copy-start.6 = (s32[5,32]{1,0:T(8,128)S(1)}, s32[5,32]{1,0:T(8,128)}, u32[]{:S(2)}) copy-start(s32[5,32]{1,0:T(8,128)} %param.10) | copy-start | bytes 1924
  16.3 39.6 %copy-start = (bf16[5,64,2048]{2,1,0:T(8,128)(2,1)S(1)}, bf16[5,64,2048]{2,1,0:T(8,128)(2,1)}, u32[]{:S(2)}) copy-start(bf16[5,64,2048]{2,1,0:T(8,128)(2,1)} %off.1) | copy-start | bytes 3932164
  16.3 39.6 %copy-start.1 = (bf16[64,2048]{1,0:T(8,128)(2,1)S(1)}, bf16[64,2048]{1,0:T(8,128)(2,1)}, u32[]{:S(2)}) copy-start(bf16[64,2048]{1,0:T(8,128)(2,1)} %diag.1) | copy-start | bytes 786436
  16.3 39.6 %copy-start.4 = (f32[2048]{0:T(1024)S(1)}, f32[2048]{0:T(1024)}, u32[]{:S(2)}) copy-start(f32[2048]{0:T(1024)} %param.7) | copy-start | bytes 24580
  17.2 38.7 %all-to-all-start.1 = ((bf16[16,4,32,128]{3,2,1,0:T(8,128)(2,1)}), bf16[16,4,32,128]{3,2,1,0:T(8,128)(2,1)S(1)}, u32[]{:S(2)}, u32[]{:S(2)}) async-start(bf16[16,4,32,128]{3,2,1,0:T(8,128)(2,1)} %copy_bitcast_fusion), calls=%async_computation.1 | async-start | bytes 1048576 | tf_op jit(solution)/shard_map/all_to_all | solution.py:162
  33.9 21.9 %collective-permute-start.1 = (bf16[4,32,128]{2,1,0:T(8,128)(2,1)S(1)}, bf16[4,32,128]{2,1,0:T(8,128)(2,1)S(1)}, u32[]{:S(2)}, u32[]{:S(2)}) collective-permute-start(bf16[4,32,128]{2,1,0:T(8,128)(2,1)S(1)} %get-tuple-element.10), channel_id=1, source_target_pairs={{4,0},{8,4},{12,8},{16,12},{20,16},{24,20},{28,24},{32,28},{36,32}... | collective-permute-start | bytes 98312 | tf_op jit(solution)/shard_map/ppermute | solution.py:161
  38.4 17.5 %collective-permute-start = (bf16[4,32,128]{2,1,0:T(8,128)(2,1)S(1)}, bf16[4,32,128]{2,1,0:T(8,128)(2,1)S(1)}, u32[]{:S(2)}, u32[]{:S(2)}) collective-permute-start(bf16[4,32,128]{2,1,0:T(8,128)(2,1)S(1)} %get-tuple-element.11), channel_id=1, source_target_pairs={{0,4},{4,8},{8,12},{12,16},{16,20},{20,24},{24,28},{28,32},{32,36}... | collective-permute-start | bytes 98312 | tf_op jit(solution)/shard_map/ppermute | solution.py:160

commit v2 on v1

--- a/solution.py
+++ b/solution.py
@@ -19,11 +19,28 @@
     return pl.BlockSpec(memory_space=pltpu.SMEM)
 
 
+def outside():
+    return pl.BlockSpec(memory_space=pltpu.HBM)
+
+
+def anywhere():
+    return pl.BlockSpec(memory_space=pl.ANY)
+
+
 def left_half(rows):
     return lax.broadcasted_iota(jnp.int32, (rows, 128), 1) < 64
 
 
-def pack_kernel(lists, panel, scale, scaled, payload, blocks):
+def pack_kernel(lists_at, panel_at, scale_at, scaled, payload, extra, lists, panel, scale, blocks, sems):
+    fetches = [
+        pltpu.make_async_copy(scale_at, scale, sems.at[0]),
+        pltpu.make_async_copy(panel_at, panel, sems.at[1]),
+        pltpu.make_async_copy(lists_at, lists, sems.at[2]),
+    ]
+    for fetch in fetches:
+        fetch.start()
+    for fetch in fetches:
+        fetch.wait()
     left = left_half(32)
     for i in range(panel.shape[1] // 128):
         cols = slice(128 * i, 128 * i + 128)
@@ -38,12 +55,12 @@
     rank = z * NX + x
     for to in range(NX):
         for zz in range(NZ):
-            payload[to, zz] = blocks[jnp.maximum(lists[zz * NX + to, 0], 0)]
+            payload[zz * NX + to] = blocks[jnp.maximum(lists[0, zz * NX + to], 0)]
         step = lax.rem(to - x + NX, NX)
         first = lax.rem(rank + step, NZ * NX)
         second = lax.rem(rank + step - NX + NZ * NX, NZ * NX)
-        payload[to, NZ] = blocks[jnp.maximum(lists[first, 1], 0)]
-        payload[to, NZ + 1] = blocks[jnp.maximum(lists[second, 1], 0)]
+        extra[jnp.bitwise_xor(to, x), 0] = blocks[jnp.maximum(lists[1, first], 0)]
+        extra[jnp.bitwise_xor(to, x), 1] = blocks[jnp.maximum(lists[1, second], 0)]
 
 
 def multiply_kernel(where_at, main, near, above, below, scaled, scale, diag, off, halves, gram, table):
@@ -56,7 +73,7 @@
         table[at, 32:] = jnp.where(left, turned, wide).astype(jnp.bfloat16)
 
     for s in range(NZ * NX):
-        spread(s, main[s // NX, s % NX])
+        spread(s, main[s])
     for s in range(NX):
         spread(64 + s, near[s, 0])
         spread(68 + s, near[s, 1])
@@ -100,23 +117,37 @@
     gram[:, 0, :] = jnp.where(left, total[:32], total[32:])
 
 
-def finish_kernel(node_count, gram, halves, basis, factor):
+def factor_rows(blocks):
+    sub = lax.broadcasted_iota(jnp.int32, (8, 128), 0)
+    for p in range(8):
+        columns = [
+            [jnp.broadcast_to(blocks[r][:, 8 * p + j : 8 * p + j + 1], (8, 128)) for r in range(p, 8)]
+            for j in range(8)
+        ]
+        for j in range(8):
+            pivot = jnp.broadcast_to(columns[j][0][j : j + 1], (8, 128))
+            inverse = lax.rsqrt(pivot)
+            inverse = inverse * (1.5 - 0.5 * pivot * inverse * inverse)
+            ratio = [c * inverse for c in columns[j]]
+            ratio[0] = jnp.where(sub > j, ratio[0], 0.0)
+            for t in range(j + 1, 8):
+                lead = jnp.broadcast_to(columns[t][0][j : j + 1], (8, 128)) * inverse
+                columns[t] = [c - f * lead for c, f in zip(columns[t], ratio)]
+            lead = jnp.broadcast_to(blocks[p][j : j + 1], (8, 128)) * inverse
+            for r in range(p, 8):
+                blocks[r] = blocks[r] - ratio[r - p] * lead
+            blocks[p] = jnp.where(sub == j, lead, blocks[p])
+    return jnp.concatenate(blocks, axis=0)
+
+
+def finish_kernel(node_count, gram, halves, basis_at, factor, basis, sems):
     packed = gram[:, 0, :] * (1.0 / node_count)
     turned = pltpu.roll(packed, 64, 1)
     full = jnp.concatenate([packed, turned], axis=0)
     lane = lax.broadcasted_iota(jnp.int32, (64, 128), 1)
     row = lax.broadcasted_iota(jnp.int32, (64, 128), 0)
     work = jnp.where(lane < 64, full, (lane - 64 == row).astype(jnp.float32))
-    for k in range(64):
-        column = jnp.broadcast_to(work[:, k : k + 1], (64, 128))
-        pivot = column[k : k + 1, :]
-        inverse = lax.rsqrt(pivot)
-        inverse = inverse * (1.5 - 0.5 * pivot * inverse * inverse)
-        scaled_row = work[k : k + 1, :] * inverse
-        factor_column = column * inverse
-        work = jnp.where(
-            row > k, work - factor_column * scaled_row, jnp.where(row == k, scaled_row, work)
-        )
+    work = factor_rows([work[8 * r : 8 * r + 8] for r in range(8)])
     factor[...] = jnp.where(row <= lane, work, 0.0)[:, :64]
     solve = pltpu.roll(work, 64, 1)
     solve = jnp.where((lane < 64) & (lane <= row), solve, 0.0)
@@ -124,42 +155,55 @@
     low = (solve - high.astype(jnp.float32)).astype(jnp.bfloat16)
     twice = jnp.where(lane < 64, solve, pltpu.roll(solve, 64, 1)).astype(jnp.bfloat16)
     left = jnp.concatenate([twice, low], axis=0)
+    stores = []
     for i in range(halves.shape[1] // 256):
         cols = slice(256 * i, 256 * i + 256)
         both = jnp.dot(left, halves[:, cols], preferred_element_type=jnp.float32)
         basis[:, cols] = both[:64] + both[64:]
+        stores.append(pltpu.make_async_copy(basis.at[:, cols], basis_at.at[:, cols], sems.at[i]))
+        stores[-1].start()
+    for store in stores:
+        store.wait()
 
 
 def shards(test_panel, node_scale, diag_blocks, off_blocks, block_columns, send_lists):
     panel_width, local_nodes = test_panel.shape
     node_count = local_nodes * NY * NC * NZ * NX
     scale = node_scale.reshape(local_nodes // 128, 128)
-    scaled, payload = pl.pallas_call(
+    scaled, payload, extra = pl.pallas_call(
         pack_kernel,
         out_shape=(
             jax.ShapeDtypeStruct((64, local_nodes), jnp.bfloat16),
-            jax.ShapeDtypeStruct((NX, NZ + 2, 32, 128), jnp.bfloat16),
+            jax.ShapeDtypeStruct((NZ * NX, 32, 128), jnp.bfloat16),
+            jax.ShapeDtypeStruct((NX, 2, 32, 128), jnp.bfloat16),
         ),
-        in_specs=[smem(), vmem(), vmem()],
-        out_specs=(vmem(), vmem()),
-        scratch_shapes=[pltpu.VMEM((32, 32, 128), jnp.bfloat16)],
-        compiler_params=pltpu.CompilerParams(vmem_limit_bytes=8 * MIB),
+        in_specs=[outside(), outside(), outside()],
+        out_specs=(vmem(), vmem(), vmem()),
+        scratch_shapes=[
+            pltpu.SMEM((2, NZ * NX), jnp.int32),
+            pltpu.VMEM((64, local_nodes), jnp.bfloat16),
+            pltpu.VMEM((local_nodes // 128, 128), jnp.float32),
+            pltpu.VMEM((32, 32, 128), jnp.bfloat16),
+            pltpu.SemaphoreType.DMA((3,)),
+        ],
         name="pack",
-    )(send_lists, test_panel, scale)
+    )(send_lists.T, test_panel, scale)
 
     z, x = lax.axis_index("z"), lax.axis_index("x")
     source, entry = block_columns // 2, block_columns % 2
     source_z, source_x = source // NX, source % NX
-    same = 64 + jnp.where(source_x <= x, source_x, NX + source_x)
-    other = jnp.where(source_z == (z + NZ - 1) % NZ, 72, 76) + source_x
+    apart = source_x ^ x
+    same = 64 + jnp.where(source_x <= x, apart, NX + apart)
+    other = jnp.where(source_z == (z + NZ - 1) % NZ, 72, 76) + apart
     where_at = jnp.where(entry == 0, source, jnp.where(source_z == z, same, other))
 
-    near = lax.all_to_all(payload, "x", 0, 0, tiled=True)
+    main = lax.all_to_all(payload, ("z", "x"), 0, 0, tiled=True)
+    moved = [lax.ppermute(extra[d], "x", [(i, i ^ d) for i in range(NX)]) for d in (1, 2, 3)]
+    near = jnp.stack([extra[0]] + moved)
     up = [(i, (i + 1) % NZ) for i in range(NZ)]
     down = [((i + 1) % NZ, i) for i in range(NZ)]
-    above = lax.ppermute(near[:, NZ], "z", up)
-    below = lax.ppermute(near[:, NZ + 1], "z", down)
-    main = lax.all_to_all(near[:, :NZ].transpose(1, 0, 2, 3), "z", 0, 0, tiled=True)
+    above = lax.ppermute(near[:, 0], "z", up)
+    below = lax.ppermute(near[:, 1], "z", down)
 
     halves, gram = pl.pallas_call(
         multiply_kernel,
@@ -172,7 +216,7 @@
         scratch_shapes=[pltpu.VMEM((80, 64, 128), jnp.bfloat16)],
         compiler_params=pltpu.CompilerParams(vmem_limit_bytes=16 * MIB),
         name="multiply",
-    )(where_at, main, near[:, NZ:], above, below, scaled, scale, diag_blocks, off_blocks)
+    )(where_at, main, near, above, below, scaled, scale, diag_blocks, off_blocks)
 
     part = lax.all_to_all(gram, PLANE, 0, 0, tiled=True).sum(0)
     part = lax.all_to_all(jnp.broadcast_to(part[None], (NZ, 1, 128)), "z", 0, 0, tiled=True).sum(0)
@@ -188,7 +232,11 @@
             jax.ShapeDtypeStruct((64, 64), jnp.float32),
         ),
         in_specs=[vmem(), vmem()],
-        out_specs=(vmem(), vmem()),
+        out_specs=(anywhere(), vmem()),
+        scratch_shapes=[
+            pltpu.VMEM((64, local_nodes), jnp.float32),
+            pltpu.SemaphoreType.DMA((local_nodes // 256,)),
+        ],
         compiler_params=pltpu.CompilerParams(vmem_limit_bytes=8 * MIB),
         name="finish",
     )(gram, halves)

time: 117 us -> 104 us (0.89)
  blocking collectives: 61.9 us -> 43.5 us
  starting transfers between devices: 23.1 us -> 34.9 us
  local copies, waits for them, and re-layouts: 4.17 us -> 1.66 us
  Pallas kernels: 11.9 us -> 9.86 us
  waiting for transfers between devices: 14.6 us -> 12.6 us
    all_to_all x1 -> x0, blocking collectives: 11.9 us -> none  [shards(): near = lax.all_to_all(payload, 'x', 0, 0, tiled=True)]
    ppermute x2 -> x5, starting transfers between devices: 6.39 us -> 15.7 us  [the longest x3 9.13 us: shards(): lax.ppermute(extra[d], 'x', [(i, i ^ d) for i in range(NX)])]
    ppermute x2 -> x5, waiting for transfers between devices: 14.6 us -> 7.79 us  [the longest x1 3.86 us: shards(): above = lax.ppermute(near[:, 0], 'z', up)]
    all_to_all x1, waiting for transfers between devices: 0.01 us -> 4.85 us  [shards(): main = lax.all_to_all(payload, ('z', 'x'), 0, 0, tiled=True)]
    all_to_all x1, blocking collectives: 17.5 us -> 13.8 us  [shards(): lax.all_to_all(jnp.broadcast_to(part[None], (NZ, 1, 128)), 'z', 0, 0, til...]
    pallas_call x1, Pallas kernels: 6.91 us -> 4 us  [shards(): pl.pallas_call(finish, out_shape=(jax.ShapeDtypeStruct((64, local_nodes),...]
    all_to_all x1, blocking collectives: 20.4 us -> 17.8 us  [shards(): part = lax.all_to_all(gram, PLANE, 0, 0, tiled=True).sum(0)]
    all_to_all x1, starting transfers between devices: 16.7 us -> 19.2 us  [shards(): main = lax.all_to_all(payload, ('z', 'x'), 0, 0, tiled=True)]
  transfers between devices with their start and end apart: 3 -> 6, of which waited for: 1 -> 4; matrix products, arithmetic and copies ran while one was open for 1% -> 2% of each run, Pallas kernels for 0% -> 0%
where the time goes in v2:
time: 104 us; the launch traced here: 103 us
  blocking collectives  43.5 us (42%)
  starting transfers between devices  34.9 us (34%)
  waiting for transfers between devices  12.6 us (12%)
  Pallas kernels  9.86 us (9%)
  local copies, waits for them, and re-layouts  1.66 us (2%)
    all_to_all x1, starting transfers between devices, shards(): main = lax.all_to_all(payload, ('z', 'x'), 0, 0, tiled=True)  19.2 us
    all_to_all x1, blocking collectives, shards(): part = lax.all_to_all(gram, PLANE, 0, 0, tiled=True).sum(0)  17.8 us
    all_to_all x1, blocking collectives, shards(): lax.all_to_all(jnp.broadcast_to(part[None], (NZ, 1, 128)), 'z', 0, 0, til...  13.8 us
    all_to_all x1, blocking collectives, shards(): lax.all_to_all(jnp.broadcast_to(part[None], (NPLANE, 1, 128)), PLANE, 0,...  11.8 us
    ppermute x3, starting transfers between devices, shards(): lax.ppermute(extra[d], 'x', [(i, i ^ d) for i in range(NX)])  9.13 us
    all_to_all x1, waiting for transfers between devices, shards(): main = lax.all_to_all(payload, ('z', 'x'), 0, 0, tiled=True)  4.85 us
    ppermute x1, starting transfers between devices, shards(): below = lax.ppermute(near[:, 1], 'z', down)  4.6 us
    pallas_call x1, Pallas kernels, shards(): pl.pallas_call(finish, out_shape=(jax.ShapeDtypeStruct((64, local_nodes),...  4 us
  transfers between devices with their start and end apart: 6, of which 4 were waited for; matrix products, arithmetic and copies ran while one was open for 2% of the time, Pallas kernels for 0%

profile of v2, /device:TPU:1, one launch (start us, length us, event | category | flops | bytes accessed | tf_op | source)
XLA Modules:
  0.0 103.5 jit_solution(919975428495841494)
XLA Ops:
  0.6 0.0 copy-start.3
  0.6 0.0 copy-start.4
  0.7 0.0 copy-start
  0.7 0.0 copy-start.1
  0.7 2.2 %pack.1 = (bf16[64,2048]{1,0:T(8,128)(2,1)}, bf16[64,32,128]{2,1,0:T(8,128)(2,1)}, bf16[4,2,32,128]{3,2,1,0:T(8,128)(2,1)}) custom-call(s32[2,64]{1,0:T(2,128)} %bitcast.22, bf16[64,2048]{1,0:T(8,128)(2,1)} %panel_at.1, f32[16,128]{1,0:T(8,128)} %bitcast.16), custom_call_target="tpu_custom_call" | custom-call | tf_op jit(solution)/shard_map/pack/pallas_call | solution.py:173
  2.9 0.0 copy-start.2
  2.9 19.2 %all-to-all-start = ((bf16[64,32,128]{2,1,0:T(8,128)(2,1)}), bf16[64,32,128]{2,1,0:T(8,128)(2,1)S(1)}, u32[]{:S(2)}, u32[]{:S(2)}) async-start(bf16[64,32,128]{2,1,0:T(8,128)(2,1)} %get-tuple-element.7), calls=%async_computation | async-start | bytes 1048576 | tf_op jit(solution)/shard_map/all_to_all | solution.py:200
  22.2 0.8 slice_bitcast_fusion.4
  22.9 2.9 %collective-permute-start = (bf16[2,32,128]{2,1,0:T(8,128)(2,1)S(1)}, bf16[2,32,128]{2,1,0:T(8,128)(2,1)S(1)}, u32[]{:S(2)}, u32[]{:S(2)}) collective-permute-start(bf16[2,32,128]{2,1,0:T(8,128)(2,1)S(1)} %get-tuple-element.14), channel_id=1, source_target_pairs={{0,1},{1,0},{2,3},{3,2},{4,5},{5,4},{6,7},{7,6},{8,9},{9,8},{10,11... | collective-permute-start | bytes 49160 | tf_op jit(solution)/shard_map/ppermute | solution.py:201
  25.8 3.7 %collective-permute-start.2 = (bf16[2,32,128]{2,1,0:T(8,128)(2,1)S(1)}, bf16[2,32,128]{2,1,0:T(8,128)(2,1)S(1)}, u32[]{:S(2)}, u32[]{:S(2)}) collective-permute-start(bf16[2,32,128]{2,1,0:T(8,128)(2,1)S(1)} %get-tuple-element.15), channel_id=1, source_target_pairs={{0,3},{1,2},{2,1},{3,0},{4,7},{5,6},{6,5},{7,4},{8,11},{9,10},{10,... | collective-permute-start | bytes 49160 | tf_op jit(solution)/shard_map/ppermute | solution.py:201
  29.5 2.5 %collective-permute-start.1 = (bf16[2,32,128]{2,1,0:T(8,128)(2,1)S(1)}, bf16[2,32,128]{2,1,0:T(8,128)(2,1)S(1)}, u32[]{:S(2)}, u32[]{:S(2)}) collective-permute-start(bf16[2,32,128]{2,1,0:T(8,128)(2,1)S(1)} %get-tuple-element.16), channel_id=1, source_target_pairs={{0,2},{1,3},{2,0},{3,1},{4,6},{5,7},{6,4},{7,5},{8,10},{9,11},{10,... | collective-permute-start | bytes 49160 | tf_op jit(solution)/shard_map/ppermute | solution.py:201
  32.1 0.8 copy.12
  32.9 0.0 collective-permute-done
  32.9 0.0 collective-permute-done.2
  33.0 2.9 %collective-permute-done.1 = bf16[2,32,128]{2,1,0:T(8,128)(2,1)S(1)} collective-permute-done((bf16[2,32,128]{2,1,0:T(8,128)(2,1)S(1)}, bf16[2,32,128]{2,1,0:T(8,128)(2,1)S(1)}, u32[]{:S(2)}, u32[]{:S(2)}) %collective-permute-start.1) | collective-permute-done | bytes 16416 | tf_op jit(solution)/shard_map/ppermute | solution.py:201
  35.9 4.6 %collective-permute-start.4 = (bf16[4,32,128]{2,1,0:T(8,128)(2,1)S(1)}, bf16[4,32,128]{2,1,0:T(8,128)(2,1)S(1)}, u32[]{:S(2)}, u32[]{:S(2)}) collective-permute-start(bf16[4,32,128]{2,1,0:T(8,128)(2,1)S(1)} %get-tuple-element.12), channel_id=1, source_target_pairs={{4,0},{8,4},{12,8},{16,12},{20,16},{24,20},{28,24},{32,28},{36,32}... | collective-permute-start | bytes 98312 | tf_op jit(solution)/shard_map/ppermute | solution.py:206
  40.5 1.9 %collective-permute-start.3 = (bf16[4,32,128]{2,1,0:T(8,128)(2,1)S(1)}, bf16[4,32,128]{2,1,0:T(8,128)(2,1)S(1)}, u32[]{:S(2)}, u32[]{:S(2)}) collective-permute-start(bf16[4,32,128]{2,1,0:T(8,128)(2,1)S(1)} %get-tuple-element.13), channel_id=1, source_target_pairs={{0,4},{4,8},{8,12},{12,16},{16,20},{20,24},{24,28},{28,32},{32,36}... | collective-permute-start | bytes 98312 | tf_op jit(solution)/shard_map/ppermute | solution.py:205
  42.4 0.0 copy-done.4
  42.5 1.0 collective-permute-done.4.below
  43.5 3.9 %collective-permute-done.3.above = bf16[4,32,128]{2,1,0:T(8,128)(2,1)S(1)} collective-permute-done((bf16[4,32,128]{2,1,0:T(8,128)(2,1)S(1)}, bf16[4,32,128]{2,1,0:T(8,128)(2,1)S(1)}, u32[]{:S(2)}, u32[]{:S(2)}) %collective-permute-start.3) | collective-permute-done | bytes 32800 | tf_op jit(solution)/shard_map/ppermute | solution.py:205
  47.4 4.8 %all-to-all-done.main = bf16[64,32,128]{2,1,0:T(8,128)(2,1)S(1)} async-done(((bf16[64,32,128]{2,1,0:T(8,128)(2,1)}), bf16[64,32,128]{2,1,0:T(8,128)(2,1)S(1)}, u32[]{:S(2)}, u32[]{:S(2)}) %all-to-all-start) | async-done | bytes 524320 | tf_op jit(solution)/shard_map/all_to_all | solution.py:200
  52.2 0.0 copy-done.3
  52.2 0.0 copy-done
  52.2 0.0 copy-done.1
  52.2 0.0 copy-done.2
  52.2 3.7 %multiply.1 = (bf16[128,2048]{1,0:T(8,128)(2,1)S(1)}, f32[32,1,128]{2,1,0:T(1,128)S(1)}) custom-call(s32[5,32]{1,0:T(8,128)S(1)} %fusion.3.where_at, bf16[64,32,128]{2,1,0:T(8,128)(2,1)S(1)} %all-to-all-done.main, bf16[4,2,32,128]{3,2,1,0:T(8,128)(2,1)S(1)} %copy.13.near, bf16[4,32,128]{2,1,0:T(8,128)(2,1)S(1)} %collective-permute-done.3.above, ...), custom_call_target="tpu_custom_call" | custom-call | tf_op jit(solution)/shard_map/multiply/pallas_call | solution.py:208
  55.9 17.8 %all_to_all.20 = f32[32,1,128]{2,1,0:T(1,128)S(1)} all-to-all(f32[32,1,128]{2,1,0:T(1,128)S(1)} %get-tuple-element.10), channel_id=1, replica_groups=mesh['y'=4,'c'=2,'z'=16,'x'=4] {'y','c','x'}, dimensions={0} | all-to-all | bytes 32768 | tf_op jit(solution)/shard_map/all_to_all | solution.py:221
  73.7 0.1 reduce_sum.18
  73.8 13.8 %all_to_all.21 = f32[16,1,128]{2,1,0:T(1,128)S(1)} all-to-all(f32[16,1,128]{2,1,0:T(1,128)S(1)} %broadcast_in_dim.22), channel_id=1, replica_groups=mesh['y'=4,'c'=2,'z'=16,'x'=4] {'z'}, dimensions={0} | all-to-all | bytes 16384 | tf_op jit(solution)/shard_map/all_to_all | solution.py:222
  87.6 11.8 %all_to_all.22.refs_0_ = f32[32,1,128]{2,1,0:T(1,128)S(1)} all-to-all(f32[32,1,128]{2,1,0:T(1,128)S(1)} %broadcast_in_dim.23), channel_id=1, replica_groups=mesh['y'=4,'c'=2,'z'=16,'x'=4] {'y','c','x'}, dimensions={0} | all-to-all | bytes 32768 | tf_op jit(solution)/shard_map/all_to_all | solution.py:223
  99.5 4.0 %finish.1 = (f32[64,2048]{1,0:T(8,128)}, f32[64,64]{1,0:T(8,128)}) custom-call(f32[32,1,128]{2,1,0:T(1,128)S(1)} %all_to_all.22.refs_0_, bf16[128,2048]{1,0:T(8,128)(2,1)S(1)} %get-tuple-element.11.refs_1_), custom_call_target="tpu_custom_call" | custom-call | tf_op jit(solution)/shard_map/finish/pallas_call | solution.py:228
  (8 shorter events, 0.1 us)
Async XLA Ops:
  0.6 51.6 %copy-start.3 = (f32[2048]{0:T(1024)S(1)}, f32[2048]{0:T(1024)}, u32[]{:S(2)}) copy-start(f32[2048]{0:T(1024)} %param.7) | copy-start | bytes 24580
  0.6 41.8 %copy-start.4 = (s32[5,32]{1,0:T(8,128)S(1)}, s32[5,32]{1,0:T(8,128)}, u32[]{:S(2)}) copy-start(s32[5,32]{1,0:T(8,128)} %param.10) | copy-start | bytes 1924
  0.7 51.6 %copy-start = (bf16[5,64,2048]{2,1,0:T(8,128)(2,1)S(1)}, bf16[5,64,2048]{2,1,0:T(8,128)(2,1)}, u32[]{:S(2)}) copy-start(bf16[5,64,2048]{2,1,0:T(8,128)(2,1)} %off.1) | copy-start | bytes 3932164
  0.7 51.6 %copy-start.1 = (bf16[64,2048]{1,0:T(8,128)(2,1)S(1)}, bf16[64,2048]{1,0:T(8,128)(2,1)}, u32[]{:S(2)}) copy-start(bf16[64,2048]{1,0:T(8,128)(2,1)} %diag.1) | copy-start | bytes 786436
  2.9 49.3 %copy-start.2 = (bf16[64,2048]{1,0:T(8,128)(2,1)S(1)}, bf16[64,2048]{1,0:T(8,128)(2,1)}, u32[]{:S(2)}) copy-start(bf16[64,2048]{1,0:T(8,128)(2,1)} %get-tuple-element.9.scaled) | copy-start | bytes 786436
  2.9 49.3 %all-to-all-start = ((bf16[64,32,128]{2,1,0:T(8,128)(2,1)}), bf16[64,32,128]{2,1,0:T(8,128)(2,1)S(1)}, u32[]{:S(2)}, u32[]{:S(2)}) async-start(bf16[64,32,128]{2,1,0:T(8,128)(2,1)} %get-tuple-element.7), calls=%async_computation | async-start | bytes 1048576 | tf_op jit(solution)/shard_map/all_to_all | solution.py:200
  22.9 10.0 %collective-permute-start = (bf16[2,32,128]{2,1,0:T(8,128)(2,1)S(1)}, bf16[2,32,128]{2,1,0:T(8,128)(2,1)S(1)}, u32[]{:S(2)}, u32[]{:S(2)}) collective-permute-start(bf16[2,32,128]{2,1,0:T(8,128)(2,1)S(1)} %get-tuple-element.14), channel_id=1, source_target_pairs={{0,1},{1,0},{2,3},{3,2},{4,5},{5,4},{6,7},{7,6},{8,9},{9,8},{10,11... | collective-permute-start | bytes 49160 | tf_op jit(solution)/shard_map/ppermute | solution.py:201
  25.8 7.1 %collective-permute-start.2 = (bf16[2,32,128]{2,1,0:T(8,128)(2,1)S(1)}, bf16[2,32,128]{2,1,0:T(8,128)(2,1)S(1)}, u32[]{:S(2)}, u32[]{:S(2)}) collective-permute-start(bf16[2,32,128]{2,1,0:T(8,128)(2,1)S(1)} %get-tuple-element.15), channel_id=1, source_target_pairs={{0,3},{1,2},{2,1},{3,0},{4,7},{5,6},{6,5},{7,4},{8,11},{9,10},{10,... | collective-permute-start | bytes 49160 | tf_op jit(solution)/shard_map/ppermute | solution.py:201
  29.5 6.3 %collective-permute-start.1 = (bf16[2,32,128]{2,1,0:T(8,128)(2,1)S(1)}, bf16[2,32,128]{2,1,0:T(8,128)(2,1)S(1)}, u32[]{:S(2)}, u32[]{:S(2)}) collective-permute-start(bf16[2,32,128]{2,1,0:T(8,128)(2,1)S(1)} %get-tuple-element.16), channel_id=1, source_target_pairs={{0,2},{1,3},{2,0},{3,1},{4,6},{5,7},{6,4},{7,5},{8,10},{9,11},{10,... | collective-permute-start | bytes 49160 | tf_op jit(solution)/shard_map/ppermute | solution.py:201
  35.9 7.6 %collective-permute-start.4 = (bf16[4,32,128]{2,1,0:T(8,128)(2,1)S(1)}, bf16[4,32,128]{2,1,0:T(8,128)(2,1)S(1)}, u32[]{:S(2)}, u32[]{:S(2)}) collective-permute-start(bf16[4,32,128]{2,1,0:T(8,128)(2,1)S(1)} %get-tuple-element.12), channel_id=1, source_target_pairs={{4,0},{8,4},{12,8},{16,12},{20,16},{24,20},{28,24},{32,28},{36,32}... | collective-permute-start | bytes 98312 | tf_op jit(solution)/shard_map/ppermute | solution.py:206
  40.5 6.9 %collective-permute-start.3 = (bf16[4,32,128]{2,1,0:T(8,128)(2,1)S(1)}, bf16[4,32,128]{2,1,0:T(8,128)(2,1)S(1)}, u32[]{:S(2)}, u32[]{:S(2)}) collective-permute-start(bf16[4,32,128]{2,1,0:T(8,128)(2,1)S(1)} %get-tuple-element.13), channel_id=1, source_target_pairs={{0,4},{4,8},{8,12},{12,16},{16,20},{20,24},{24,28},{28,32},{32,36}... | collective-permute-start | bytes 98312 | tf_op jit(solution)/shard_map/ppermute | solution.py:205

commit v3 on v2

--- a/solution.py
+++ b/solution.py
@@ -47,8 +47,9 @@
         slab = panel[:, cols].astype(jnp.float32) * scale[i : i + 1, :]
         scaled[:, cols] = slab.astype(jnp.bfloat16)
         top, low = slab[:32], slab[32:]
-        even = jnp.where(left, top, pltpu.roll(low, 64, 1))
-        odd = jnp.where(left, pltpu.roll(top, 64, 1), low)
+        turned = pltpu.roll(slab, 64, 1)
+        even = jnp.where(left, top, turned[32:])
+        odd = jnp.where(left, turned[:32], low)
         blocks[2 * i] = even.astype(jnp.bfloat16)
         blocks[2 * i + 1] = odd.astype(jnp.bfloat16)
     z, x = lax.axis_index("z"), lax.axis_index("x")
@@ -81,40 +82,53 @@
         spread(76 + s, below[s])
 
     left64 = left_half(64)
-    same = (lax.broadcasted_iota(jnp.int32, (128, 128), 0) < 64) == left_half(128)
-    zero = jnp.zeros((), jnp.bfloat16)
-    total = jnp.zeros((128, 128), jnp.float32)
     for i in range(scaled.shape[1] // 128):
         cols = slice(128 * i, 128 * i + 128)
-        own = diag[:, cols]
-        own = jnp.where(same, jnp.concatenate([own, own], axis=0), zero)
-        product = jnp.dot(scaled[:, cols], own, preferred_element_type=jnp.float32)
         rows = []
-        for b in (2 * i, 2 * i + 1):
+        own = scaled[:, cols]
+        swapped = pltpu.roll(own, 64, 1)
+        for b, side in ((2 * i, swapped), (2 * i + 1, own)):
             read = [table[where_at[k, b]] for k in range(5)]
             first = jnp.where(left64, read[0], read[1])
             second = jnp.where(left64, read[2], read[3])
-            third = jnp.where(left64, read[4], zero)
+            third = jnp.where(left64, read[4], side)
             rows.append(jnp.concatenate([first, second, third], axis=1))
         weights = [off[k, :, cols] for k in range(5)]
-        weights.append(jnp.zeros((64, 128), jnp.bfloat16))
+        weights.append(diag[:, cols])
         both = jnp.dot(
             jnp.concatenate(rows, axis=0),
             jnp.concatenate(weights, axis=0),
             preferred_element_type=jnp.float32,
         )
-        product = product + jnp.where(left64, both[:64], both[64:])
+        product = jnp.where(left64, both[:64], both[64:])
         sketch = product * scale[i : i + 1, :]
         high = sketch.astype(jnp.bfloat16)
         low = (sketch - high.astype(jnp.float32)).astype(jnp.bfloat16)
         pair = jnp.concatenate([high, low], axis=0)
         halves[:, cols] = pair
-        total = total + lax.dot_general(
-            pair, pair, (((1,), (1,)), ((), ())), preferred_element_type=jnp.float32
-        )
+    every = halves[...]
+    total = lax.dot_general(every, every, (((1,), (1,)), ((), ())), preferred_element_type=jnp.float32)
     total = total[:64] + total[64:]
     total = total + pltpu.roll(total, 64, 1)
-    gram[:, 0, :] = jnp.where(left, total[:32], total[32:])
+    lane = lax.broadcasted_iota(jnp.int32, (32, 128), 1)
+    row = lax.broadcasted_iota(jnp.int32, (32, 128), 0)
+    folded = jnp.where((lane & 63) <= row, total[:32], pltpu.roll(total[32:], 32, 1))
+    gram[:16] = jnp.where(lane[:16] < 64, folded[:16], folded[16:])
+    corner = jnp.where(lane == row + 32, total[32:], 0.0)
+    gram[16:] = jnp.sum(corner, axis=0, keepdims=True)
+
+
+def unfold(packed):
+    lane = lax.broadcasted_iota(jnp.int32, (32, 128), 1)
+    row = lax.broadcasted_iota(jnp.int32, (32, 128), 0)
+    folded = jnp.concatenate([packed[:16], pltpu.roll(packed[:16], 64, 1)], axis=0)
+    turned = jnp.concatenate([folded, jnp.zeros((96, 128), jnp.float32)], axis=0).T
+    across = jnp.where(lane < 32, turned[:32], pltpu.roll(turned[32:64], 32, 1))
+    top = jnp.where(lane <= row, folded, across)
+    corner = jnp.where(lane == row + 32, packed[16:], pltpu.roll(turned[:32], 32, 1))
+    corner = jnp.where(lane > row + 32, pltpu.roll(folded, 32, 1), corner)
+    low = jnp.where(lane < 32, pltpu.roll(folded, 96, 1), corner)
+    return jnp.concatenate([top, low], axis=0)
 
 
 def factor_rows(blocks):
@@ -127,7 +141,6 @@
         for j in range(8):
             pivot = jnp.broadcast_to(columns[j][0][j : j + 1], (8, 128))
             inverse = lax.rsqrt(pivot)
-            inverse = inverse * (1.5 - 0.5 * pivot * inverse * inverse)
             ratio = [c * inverse for c in columns[j]]
             ratio[0] = jnp.where(sub > j, ratio[0], 0.0)
             for t in range(j + 1, 8):
@@ -141,9 +154,7 @@
 
 
 def finish_kernel(node_count, gram, halves, basis_at, factor, basis, sems):
-    packed = gram[:, 0, :] * (1.0 / node_count)
-    turned = pltpu.roll(packed, 64, 1)
-    full = jnp.concatenate([packed, turned], axis=0)
+    full = unfold(gram[...] * (1.0 / node_count))
     lane = lax.broadcasted_iota(jnp.int32, (64, 128), 1)
     row = lax.broadcasted_iota(jnp.int32, (64, 128), 0)
     work = jnp.where(lane < 64, full, (lane - 64 == row).astype(jnp.float32))
@@ -209,7 +220,7 @@
         multiply_kernel,
         out_shape=(
             jax.ShapeDtypeStruct((128, local_nodes), jnp.bfloat16),
-            jax.ShapeDtypeStruct((32, 1, 128), jnp.float32),
+            jax.ShapeDtypeStruct((17, 128), jnp.float32),
         ),
         in_specs=[smem()] + [vmem()] * 8,
         out_specs=(vmem(), vmem()),
@@ -218,9 +229,11 @@
         name="multiply",
     )(where_at, main, near, above, below, scaled, scale, diag_blocks, off_blocks)
 
-    part = lax.all_to_all(gram, PLANE, 0, 0, tiled=True).sum(0)
-    part = lax.all_to_all(jnp.broadcast_to(part[None], (NZ, 1, 128)), "z", 0, 0, tiled=True).sum(0)
-    gram = lax.all_to_all(jnp.broadcast_to(part[None], (NPLANE, 1, 128)), PLANE, 0, 0, tiled=True)
+    def summed(part, axes, count):
+        copies = jnp.broadcast_to(part[None, :, None], (count, 17, 1, 128))
+        return lax.all_to_all(copies, axes, 0, 0, tiled=True).sum((0, 2))
+
+    gram = summed(summed(gram, PLANE, NPLANE), "z", NZ)
 
     def finish(*refs):
         finish_kernel(node_count, *refs)

time: 104 us -> 95 us (0.913)
  blocking collectives: 43.5 us -> 35.2 us
  Pallas kernels: 9.86 us -> 7.95 us
    all_to_all x3 -> x2, blocking collectives: 43.5 us -> 35.2 us  [summed(): return lax.all_to_all(copies, axes, 0, 0, tiled=True).sum((0, 2))]
    pallas_call x1, Pallas kernels: 3.65 us -> 2.02 us  [shards(): pl.pallas_call(multiply_kernel, out_shape=(jax.ShapeDtypeStruct((128, loc...]
where the time goes in v3:
time: 95 us; the launch traced here: 93.6 us
  blocking collectives  35.2 us (37%)
  starting transfers between devices  34.9 us (37%)
  waiting for transfers between devices  12.6 us (13%)
  Pallas kernels  7.95 us (8%)
  local copies, waits for them, and re-layouts  1.86 us (2%)
    all_to_all x2, blocking collectives, summed(): return lax.all_to_all(copies, axes, 0, 0, tiled=True).sum((0, 2))  35.2 us
    all_to_all x1, starting transfers between devices, shards(): main = lax.all_to_all(payload, ('z', 'x'), 0, 0, tiled=True)  19.3 us
    ppermute x3, starting transfers between devices, shards(): lax.ppermute(extra[d], 'x', [(i, i ^ d) for i in range(NX)])  9.13 us
    all_to_all x1, waiting for transfers between devices, shards(): main = lax.all_to_all(payload, ('z', 'x'), 0, 0, tiled=True)  4.85 us
    ppermute x1, starting transfers between devices, shards(): below = lax.ppermute(near[:, 1], 'z', down)  4.6 us
    ppermute x1, waiting for transfers between devices, shards(): above = lax.ppermute(near[:, 0], 'z', up)  3.86 us
    pallas_call x1, Pallas kernels, shards(): pl.pallas_call(finish, out_shape=(jax.ShapeDtypeStruct((64, local_nodes),...  3.72 us
    ppermute x3, waiting for transfers between devices, shards(): lax.ppermute(extra[d], 'x', [(i, i ^ d) for i in range(NX)])  2.91 us
  transfers between devices with their start and end apart: 6, of which 4 were waited for; matrix products, arithmetic and copies ran while one was open for 2% of the time, Pallas kernels for 0%

profile of v3, /device:TPU:1, one launch (start us, length us, event | category | flops | bytes accessed | tf_op | source)
XLA Modules:
  0.0 93.6 jit_solution(3111739545127997171)
XLA Ops:
  0.6 0.0 copy-start.3
  0.6 0.0 copy-start.4
  0.7 0.0 copy-start
  0.7 0.0 copy-start.1
  0.7 2.2 %pack.1 = (bf16[64,2048]{1,0:T(8,128)(2,1)}, bf16[64,32,128]{2,1,0:T(8,128)(2,1)}, bf16[4,2,32,128]{3,2,1,0:T(8,128)(2,1)}) custom-call(s32[2,64]{1,0:T(2,128)} %bitcast.20, bf16[64,2048]{1,0:T(8,128)(2,1)} %panel_at.1, f32[16,128]{1,0:T(8,128)} %bitcast.15), custom_call_target="tpu_custom_call" | custom-call | tf_op jit(solution)/shard_map/pack/pallas_call | solution.py:184
  2.9 0.0 copy-start.2
  2.9 19.3 %all-to-all-start = ((bf16[64,32,128]{2,1,0:T(8,128)(2,1)}), bf16[64,32,128]{2,1,0:T(8,128)(2,1)S(1)}, u32[]{:S(2)}, u32[]{:S(2)}) async-start(bf16[64,32,128]{2,1,0:T(8,128)(2,1)} %get-tuple-element.7), calls=%async_computation | async-start | bytes 1048576 | tf_op jit(solution)/shard_map/all_to_all | solution.py:211
  22.2 0.8 slice_bitcast_fusion.4
  22.9 2.9 %collective-permute-start = (bf16[2,32,128]{2,1,0:T(8,128)(2,1)S(1)}, bf16[2,32,128]{2,1,0:T(8,128)(2,1)S(1)}, u32[]{:S(2)}, u32[]{:S(2)}) collective-permute-start(bf16[2,32,128]{2,1,0:T(8,128)(2,1)S(1)} %get-tuple-element.14), channel_id=1, source_target_pairs={{0,1},{1,0},{2,3},{3,2},{4,5},{5,4},{6,7},{7,6},{8,9},{9,8},{10,11... | collective-permute-start | bytes 49160 | tf_op jit(solution)/shard_map/ppermute | solution.py:212
  25.8 3.7 %collective-permute-start.2 = (bf16[2,32,128]{2,1,0:T(8,128)(2,1)S(1)}, bf16[2,32,128]{2,1,0:T(8,128)(2,1)S(1)}, u32[]{:S(2)}, u32[]{:S(2)}) collective-permute-start(bf16[2,32,128]{2,1,0:T(8,128)(2,1)S(1)} %get-tuple-element.15), channel_id=1, source_target_pairs={{0,3},{1,2},{2,1},{3,0},{4,7},{5,6},{6,5},{7,4},{8,11},{9,10},{10,... | collective-permute-start | bytes 49160 | tf_op jit(solution)/shard_map/ppermute | solution.py:212
  29.5 2.5 %collective-permute-start.1 = (bf16[2,32,128]{2,1,0:T(8,128)(2,1)S(1)}, bf16[2,32,128]{2,1,0:T(8,128)(2,1)S(1)}, u32[]{:S(2)}, u32[]{:S(2)}) collective-permute-start(bf16[2,32,128]{2,1,0:T(8,128)(2,1)S(1)} %get-tuple-element.16), channel_id=1, source_target_pairs={{0,2},{1,3},{2,0},{3,1},{4,6},{5,7},{6,4},{7,5},{8,10},{9,11},{10,... | collective-permute-start | bytes 49160 | tf_op jit(solution)/shard_map/ppermute | solution.py:212
  32.1 0.8 copy.12
  32.9 0.0 collective-permute-done
  32.9 0.0 collective-permute-done.2
  33.0 2.9 %collective-permute-done.1 = bf16[2,32,128]{2,1,0:T(8,128)(2,1)S(1)} collective-permute-done((bf16[2,32,128]{2,1,0:T(8,128)(2,1)S(1)}, bf16[2,32,128]{2,1,0:T(8,128)(2,1)S(1)}, u32[]{:S(2)}, u32[]{:S(2)}) %collective-permute-start.1) | collective-permute-done | bytes 16416 | tf_op jit(solution)/shard_map/ppermute | solution.py:212
  35.9 4.6 %collective-permute-start.4 = (bf16[4,32,128]{2,1,0:T(8,128)(2,1)S(1)}, bf16[4,32,128]{2,1,0:T(8,128)(2,1)S(1)}, u32[]{:S(2)}, u32[]{:S(2)}) collective-permute-start(bf16[4,32,128]{2,1,0:T(8,128)(2,1)S(1)} %get-tuple-element.12), channel_id=1, source_target_pairs={{4,0},{8,4},{12,8},{16,12},{20,16},{24,20},{28,24},{32,28},{36,32}... | collective-permute-start | bytes 98312 | tf_op jit(solution)/shard_map/ppermute | solution.py:217
  40.5 1.9 %collective-permute-start.3 = (bf16[4,32,128]{2,1,0:T(8,128)(2,1)S(1)}, bf16[4,32,128]{2,1,0:T(8,128)(2,1)S(1)}, u32[]{:S(2)}, u32[]{:S(2)}) collective-permute-start(bf16[4,32,128]{2,1,0:T(8,128)(2,1)S(1)} %get-tuple-element.13), channel_id=1, source_target_pairs={{0,4},{4,8},{8,12},{12,16},{16,20},{20,24},{24,28},{28,32},{32,36}... | collective-permute-start | bytes 98312 | tf_op jit(solution)/shard_map/ppermute | solution.py:216
  42.4 0.0 copy-done.4
  42.5 1.0 %collective-permute-done.4.below = bf16[4,32,128]{2,1,0:T(8,128)(2,1)S(1)} collective-permute-done((bf16[4,32,128]{2,1,0:T(8,128)(2,1)S(1)}, bf16[4,32,128]{2,1,0:T(8,128)(2,1)S(1)}, u32[]{:S(2)}, u32[]{:S(2)}) %collective-permute-start.4) | collective-permute-done | bytes 32800 | tf_op jit(solution)/shard_map/ppermute | solution.py:217
  43.5 3.9 %collective-permute-done.3.above = bf16[4,32,128]{2,1,0:T(8,128)(2,1)S(1)} collective-permute-done((bf16[4,32,128]{2,1,0:T(8,128)(2,1)S(1)}, bf16[4,32,128]{2,1,0:T(8,128)(2,1)S(1)}, u32[]{:S(2)}, u32[]{:S(2)}) %collective-permute-start.3) | collective-permute-done | bytes 32800 | tf_op jit(solution)/shard_map/ppermute | solution.py:216
  47.4 4.8 %all-to-all-done.main = bf16[64,32,128]{2,1,0:T(8,128)(2,1)S(1)} async-done(((bf16[64,32,128]{2,1,0:T(8,128)(2,1)}), bf16[64,32,128]{2,1,0:T(8,128)(2,1)S(1)}, u32[]{:S(2)}, u32[]{:S(2)}) %all-to-all-start) | async-done | bytes 524320 | tf_op jit(solution)/shard_map/all_to_all | solution.py:211
  52.2 0.0 copy-done.3
  52.2 0.0 copy-done
  52.2 0.0 copy-done.1
  52.2 0.0 copy-done.2
  52.2 2.0 %multiply.1 = (bf16[128,2048]{1,0:T(8,128)(2,1)S(1)}, f32[17,128]{1,0:T(8,128)S(1)}) custom-call(s32[5,32]{1,0:T(8,128)S(1)} %fusion.3.where_at, bf16[64,32,128]{2,1,0:T(8,128)(2,1)S(1)} %all-to-all-done.main, bf16[4,2,32,128]{3,2,1,0:T(8,128)(2,1)S(1)} %copy.13.near, bf16[4,32,128]{2,1,0:T(8,128)(2,1)S(1)} %collective-permute-done.3.above, ...), custom_call_target="tpu_custom_call" | custom-call | tf_op jit(solution)/shard_map/multiply/pallas_call | solution.py:219
  54.3 0.1 broadcast_in_dim.22
  54.4 20.0 %all_to_all.15 = f32[32,17,1,128]{3,2,1,0:T(1,128)S(1)} all-to-all(f32[32,17,1,128]{3,2,1,0:T(1,128)S(1)} %broadcast_in_dim.22), channel_id=1, replica_groups=mesh['y'=4,'c'=2,'z'=16,'x'=4] {'y','c','x'}, dimensions={0} | all-to-all | bytes 557056 | tf_op jit(solution)/shard_map/all_to_all | solution.py:234
  74.4 0.2 reduce_sum.18
  74.5 0.1 broadcast_in_dim.23
  74.6 15.2 %all_to_all.16 = f32[16,17,1,128]{3,2,1,0:T(1,128)S(1)} all-to-all(f32[16,17,1,128]{3,2,1,0:T(1,128)S(1)} %broadcast_in_dim.23), channel_id=1, replica_groups=mesh['y'=4,'c'=2,'z'=16,'x'=4] {'z'}, dimensions={0} | all-to-all | bytes 278528 | tf_op jit(solution)/shard_map/all_to_all | solution.py:234
  89.8 0.1 reduce_sum.19.refs_0_
  89.9 3.7 %finish.1 = (f32[64,2048]{1,0:T(8,128)}, f32[64,64]{1,0:T(8,128)}) custom-call(f32[17,128]{1,0:T(8,128)S(1)} %reduce_sum.19.refs_0_, bf16[128,2048]{1,0:T(8,128)(2,1)S(1)} %get-tuple-element.11.refs_1_), custom_call_target="tpu_custom_call" | custom-call | tf_op jit(solution)/shard_map/finish/pallas_call | solution.py:241
  (5 shorter events, 0.1 us)
Async XLA Ops:
  0.6 51.6 %copy-start.3 = (f32[2048]{0:T(1024)S(1)}, f32[2048]{0:T(1024)}, u32[]{:S(2)}) copy-start(f32[2048]{0:T(1024)} %param.7) | copy-start | bytes 24580
  0.6 41.8 %copy-start.4 = (s32[5,32]{1,0:T(8,128)S(1)}, s32[5,32]{1,0:T(8,128)}, u32[]{:S(2)}) copy-start(s32[5,32]{1,0:T(8,128)} %param.10) | copy-start | bytes 1924
  0.7 51.6 %copy-start = (bf16[5,64,2048]{2,1,0:T(8,128)(2,1)S(1)}, bf16[5,64,2048]{2,1,0:T(8,128)(2,1)}, u32[]{:S(2)}) copy-start(bf16[5,64,2048]{2,1,0:T(8,128)(2,1)} %off.1) | copy-start | bytes 3932164
  0.7 51.6 %copy-start.1 = (bf16[64,2048]{1,0:T(8,128)(2,1)S(1)}, bf16[64,2048]{1,0:T(8,128)(2,1)}, u32[]{:S(2)}) copy-start(bf16[64,2048]{1,0:T(8,128)(2,1)} %diag.1) | copy-start | bytes 786436
  2.9 49.3 %copy-start.2 = (bf16[64,2048]{1,0:T(8,128)(2,1)S(1)}, bf16[64,2048]{1,0:T(8,128)(2,1)}, u32[]{:S(2)}) copy-start(bf16[64,2048]{1,0:T(8,128)(2,1)} %get-tuple-element.9.scaled) | copy-start | bytes 786436
  2.9 49.3 %all-to-all-start = ((bf16[64,32,128]{2,1,0:T(8,128)(2,1)}), bf16[64,32,128]{2,1,0:T(8,128)(2,1)S(1)}, u32[]{:S(2)}, u32[]{:S(2)}) async-start(bf16[64,32,128]{2,1,0:T(8,128)(2,1)} %get-tuple-element.7), calls=%async_computation | async-start | bytes 1048576 | tf_op jit(solution)/shard_map/all_to_all | solution.py:211
  22.9 10.0 %collective-permute-start = (bf16[2,32,128]{2,1,0:T(8,128)(2,1)S(1)}, bf16[2,32,128]{2,1,0:T(8,128)(2,1)S(1)}, u32[]{:S(2)}, u32[]{:S(2)}) collective-permute-start(bf16[2,32,128]{2,1,0:T(8,128)(2,1)S(1)} %get-tuple-element.14), channel_id=1, source_target_pairs={{0,1},{1,0},{2,3},{3,2},{4,5},{5,4},{6,7},{7,6},{8,9},{9,8},{10,11... | collective-permute-start | bytes 49160 | tf_op jit(solution)/shard_map/ppermute | solution.py:212
  25.8 7.1 %collective-permute-start.2 = (bf16[2,32,128]{2,1,0:T(8,128)(2,1)S(1)}, bf16[2,32,128]{2,1,0:T(8,128)(2,1)S(1)}, u32[]{:S(2)}, u32[]{:S(2)}) collective-permute-start(bf16[2,32,128]{2,1,0:T(8,128)(2,1)S(1)} %get-tuple-element.15), channel_id=1, source_target_pairs={{0,3},{1,2},{2,1},{3,0},{4,7},{5,6},{6,5},{7,4},{8,11},{9,10},{10,... | collective-permute-start | bytes 49160 | tf_op jit(solution)/shard_map/ppermute | solution.py:212
  29.5 6.3 %collective-permute-start.1 = (bf16[2,32,128]{2,1,0:T(8,128)(2,1)S(1)}, bf16[2,32,128]{2,1,0:T(8,128)(2,1)S(1)}, u32[]{:S(2)}, u32[]{:S(2)}) collective-permute-start(bf16[2,32,128]{2,1,0:T(8,128)(2,1)S(1)} %get-tuple-element.16), channel_id=1, source_target_pairs={{0,2},{1,3},{2,0},{3,1},{4,6},{5,7},{6,4},{7,5},{8,10},{9,11},{10,... | collective-permute-start | bytes 49160 | tf_op jit(solution)/shard_map/ppermute | solution.py:212
  35.9 7.6 %collective-permute-start.4 = (bf16[4,32,128]{2,1,0:T(8,128)(2,1)S(1)}, bf16[4,32,128]{2,1,0:T(8,128)(2,1)S(1)}, u32[]{:S(2)}, u32[]{:S(2)}) collective-permute-start(bf16[4,32,128]{2,1,0:T(8,128)(2,1)S(1)} %get-tuple-element.12), channel_id=1, source_target_pairs={{4,0},{8,4},{12,8},{16,12},{20,16},{24,20},{28,24},{32,28},{36,32}... | collective-permute-start | bytes 98312 | tf_op jit(solution)/shard_map/ppermute | solution.py:217
  40.5 6.9 %collective-permute-start.3 = (bf16[4,32,128]{2,1,0:T(8,128)(2,1)S(1)}, bf16[4,32,128]{2,1,0:T(8,128)(2,1)S(1)}, u32[]{:S(2)}, u32[]{:S(2)}) collective-permute-start(bf16[4,32,128]{2,1,0:T(8,128)(2,1)S(1)} %get-tuple-element.13), channel_id=1, source_target_pairs={{0,4},{4,8},{8,12},{12,16},{16,20},{20,24},{24,28},{28,32},{32,36}... | collective-permute-start | bytes 98312 | tf_op jit(solution)/shard_map/ppermute | solution.py:216

commit v4 on v3

--- a/solution.py
+++ b/solution.py
@@ -131,11 +131,11 @@
     return jnp.concatenate([top, low], axis=0)
 
 
-def factor_rows(blocks):
+def factor_rows(blocks, nothing):
     sub = lax.broadcasted_iota(jnp.int32, (8, 128), 0)
     for p in range(8):
         columns = [
-            [jnp.broadcast_to(blocks[r][:, 8 * p + j : 8 * p + j + 1], (8, 128)) for r in range(p, 8)]
+            [blocks[r][:, 8 * p + j : 8 * p + j + 1] + nothing for r in range(p, 8)]
             for j in range(8)
         ]
         for j in range(8):
@@ -153,20 +153,21 @@
     return jnp.concatenate(blocks, axis=0)
 
 
-def finish_kernel(node_count, gram, halves, basis_at, factor, basis, sems):
+def finish_kernel(node_count, gram, halves, basis_at, factor_at, basis, factor, sems):
     full = unfold(gram[...] * (1.0 / node_count))
     lane = lax.broadcasted_iota(jnp.int32, (64, 128), 1)
     row = lax.broadcasted_iota(jnp.int32, (64, 128), 0)
     work = jnp.where(lane < 64, full, (lane - 64 == row).astype(jnp.float32))
-    work = factor_rows([work[8 * r : 8 * r + 8] for r in range(8)])
+    work = factor_rows([work[8 * r : 8 * r + 8] for r in range(8)], full[:8] * 0.0)
     factor[...] = jnp.where(row <= lane, work, 0.0)[:, :64]
+    stores = [pltpu.make_async_copy(factor, factor_at, sems.at[halves.shape[1] // 256])]
+    stores[0].start()
     solve = pltpu.roll(work, 64, 1)
     solve = jnp.where((lane < 64) & (lane <= row), solve, 0.0)
     high = solve.astype(jnp.bfloat16)
     low = (solve - high.astype(jnp.float32)).astype(jnp.bfloat16)
     twice = jnp.where(lane < 64, solve, pltpu.roll(solve, 64, 1)).astype(jnp.bfloat16)
     left = jnp.concatenate([twice, low], axis=0)
-    stores = []
     for i in range(halves.shape[1] // 256):
         cols = slice(256 * i, 256 * i + 256)
         both = jnp.dot(left, halves[:, cols], preferred_element_type=jnp.float32)
@@ -245,10 +246,11 @@
             jax.ShapeDtypeStruct((64, 64), jnp.float32),
         ),
         in_specs=[vmem(), vmem()],
-        out_specs=(anywhere(), vmem()),
+        out_specs=(anywhere(), anywhere()),
         scratch_shapes=[
             pltpu.VMEM((64, local_nodes), jnp.float32),
-            pltpu.SemaphoreType.DMA((local_nodes // 256,)),
+            pltpu.VMEM((64, 64), jnp.float32),
+            pltpu.SemaphoreType.DMA((local_nodes // 256 + 1,)),
         ],
         compiler_params=pltpu.CompilerParams(vmem_limit_bytes=8 * MIB),
         name="finish",

time: 95 us -> 94.2 us (level)
  no operation moved by 1% of the time
where the time goes in v4:
time: 94.2 us; the launch traced here: 92.9 us
  blocking collectives  35.2 us (37%)
  starting transfers between devices  34.9 us (37%)
  waiting for transfers between devices  12.6 us (13%)
  Pallas kernels  7.19 us (8%)
  local copies, waits for them, and re-layouts  1.86 us (2%)
    all_to_all x2, blocking collectives, summed(): return lax.all_to_all(copies, axes, 0, 0, tiled=True).sum((0, 2))  35.2 us
    all_to_all x1, starting transfers between devices, shards(): main = lax.all_to_all(payload, ('z', 'x'), 0, 0, tiled=True)  19.3 us
    ppermute x3, starting transfers between devices, shards(): lax.ppermute(extra[d], 'x', [(i, i ^ d) for i in range(NX)])  9.13 us
    all_to_all x1, waiting for transfers between devices, shards(): main = lax.all_to_all(payload, ('z', 'x'), 0, 0, tiled=True)  4.84 us
    ppermute x1, starting transfers between devices, shards(): below = lax.ppermute(near[:, 1], 'z', down)  4.61 us
    ppermute x1, waiting for transfers between devices, shards(): above = lax.ppermute(near[:, 0], 'z', up)  3.87 us
    pallas_call x1, Pallas kernels, shards(): pl.pallas_call(finish, out_shape=(jax.ShapeDtypeStruct((64, local_nodes),...  2.95 us
    ppermute x3, waiting for transfers between devices, shards(): lax.ppermute(extra[d], 'x', [(i, i ^ d) for i in range(NX)])  2.91 us
  transfers between devices with their start and end apart: 6, of which 4 were waited for; matrix products, arithmetic and copies ran while one was open for 2% of the time, Pallas kernels for 0%

profile of v4, /device:TPU:1, one launch (start us, length us, event | category | flops | bytes accessed | tf_op | source)
XLA Modules:
  0.0 92.9 jit_solution(5634546179521973948)
XLA Ops:
  0.6 0.0 copy-start.3
  0.6 0.0 copy-start.4
  0.7 0.0 copy-start
  0.7 0.0 copy-start.1
  0.7 2.2 %pack.1 = (bf16[64,2048]{1,0:T(8,128)(2,1)}, bf16[64,32,128]{2,1,0:T(8,128)(2,1)}, bf16[4,2,32,128]{3,2,1,0:T(8,128)(2,1)}) custom-call(s32[2,64]{1,0:T(2,128)} %bitcast.20, bf16[64,2048]{1,0:T(8,128)(2,1)} %panel_at.1, f32[16,128]{1,0:T(8,128)} %bitcast.15), custom_call_target="tpu_custom_call" | custom-call | tf_op jit(solution)/shard_map/pack/pallas_call | solution.py:185
  2.9 0.0 copy-start.2
  2.9 19.3 %all-to-all-start = ((bf16[64,32,128]{2,1,0:T(8,128)(2,1)}), bf16[64,32,128]{2,1,0:T(8,128)(2,1)S(1)}, u32[]{:S(2)}, u32[]{:S(2)}) async-start(bf16[64,32,128]{2,1,0:T(8,128)(2,1)} %get-tuple-element.7), calls=%async_computation | async-start | bytes 1048576 | tf_op jit(solution)/shard_map/all_to_all | solution.py:212
  22.2 0.8 slice_bitcast_fusion.4
  22.9 2.9 %collective-permute-start = (bf16[2,32,128]{2,1,0:T(8,128)(2,1)S(1)}, bf16[2,32,128]{2,1,0:T(8,128)(2,1)S(1)}, u32[]{:S(2)}, u32[]{:S(2)}) collective-permute-start(bf16[2,32,128]{2,1,0:T(8,128)(2,1)S(1)} %get-tuple-element.14), channel_id=1, source_target_pairs={{0,1},{1,0},{2,3},{3,2},{4,5},{5,4},{6,7},{7,6},{8,9},{9,8},{10,11... | collective-permute-start | bytes 49160 | tf_op jit(solution)/shard_map/ppermute | solution.py:213
  25.8 3.7 %collective-permute-start.2 = (bf16[2,32,128]{2,1,0:T(8,128)(2,1)S(1)}, bf16[2,32,128]{2,1,0:T(8,128)(2,1)S(1)}, u32[]{:S(2)}, u32[]{:S(2)}) collective-permute-start(bf16[2,32,128]{2,1,0:T(8,128)(2,1)S(1)} %get-tuple-element.15), channel_id=1, source_target_pairs={{0,3},{1,2},{2,1},{3,0},{4,7},{5,6},{6,5},{7,4},{8,11},{9,10},{10,... | collective-permute-start | bytes 49160 | tf_op jit(solution)/shard_map/ppermute | solution.py:213
  29.5 2.5 %collective-permute-start.1 = (bf16[2,32,128]{2,1,0:T(8,128)(2,1)S(1)}, bf16[2,32,128]{2,1,0:T(8,128)(2,1)S(1)}, u32[]{:S(2)}, u32[]{:S(2)}) collective-permute-start(bf16[2,32,128]{2,1,0:T(8,128)(2,1)S(1)} %get-tuple-element.16), channel_id=1, source_target_pairs={{0,2},{1,3},{2,0},{3,1},{4,6},{5,7},{6,4},{7,5},{8,10},{9,11},{10,... | collective-permute-start | bytes 49160 | tf_op jit(solution)/shard_map/ppermute | solution.py:213
  32.1 0.8 copy.12
  32.9 0.0 collective-permute-done
  32.9 0.0 collective-permute-done.2
  33.0 2.9 %collective-permute-done.1 = bf16[2,32,128]{2,1,0:T(8,128)(2,1)S(1)} collective-permute-done((bf16[2,32,128]{2,1,0:T(8,128)(2,1)S(1)}, bf16[2,32,128]{2,1,0:T(8,128)(2,1)S(1)}, u32[]{:S(2)}, u32[]{:S(2)}) %collective-permute-start.1) | collective-permute-done | bytes 16416 | tf_op jit(solution)/shard_map/ppermute | solution.py:213
  35.9 4.6 %collective-permute-start.4 = (bf16[4,32,128]{2,1,0:T(8,128)(2,1)S(1)}, bf16[4,32,128]{2,1,0:T(8,128)(2,1)S(1)}, u32[]{:S(2)}, u32[]{:S(2)}) collective-permute-start(bf16[4,32,128]{2,1,0:T(8,128)(2,1)S(1)} %get-tuple-element.12), channel_id=1, source_target_pairs={{4,0},{8,4},{12,8},{16,12},{20,16},{24,20},{28,24},{32,28},{36,32}... | collective-permute-start | bytes 98312 | tf_op jit(solution)/shard_map/ppermute | solution.py:218
  40.5 1.9 %collective-permute-start.3 = (bf16[4,32,128]{2,1,0:T(8,128)(2,1)S(1)}, bf16[4,32,128]{2,1,0:T(8,128)(2,1)S(1)}, u32[]{:S(2)}, u32[]{:S(2)}) collective-permute-start(bf16[4,32,128]{2,1,0:T(8,128)(2,1)S(1)} %get-tuple-element.13), channel_id=1, source_target_pairs={{0,4},{4,8},{8,12},{12,16},{16,20},{20,24},{24,28},{28,32},{32,36}... | collective-permute-start | bytes 98312 | tf_op jit(solution)/shard_map/ppermute | solution.py:217
  42.4 0.0 copy-done.4
  42.5 1.0 %collective-permute-done.4.below = bf16[4,32,128]{2,1,0:T(8,128)(2,1)S(1)} collective-permute-done((bf16[4,32,128]{2,1,0:T(8,128)(2,1)S(1)}, bf16[4,32,128]{2,1,0:T(8,128)(2,1)S(1)}, u32[]{:S(2)}, u32[]{:S(2)}) %collective-permute-start.4) | collective-permute-done | bytes 32800 | tf_op jit(solution)/shard_map/ppermute | solution.py:218
  43.5 3.9 %collective-permute-done.3.above = bf16[4,32,128]{2,1,0:T(8,128)(2,1)S(1)} collective-permute-done((bf16[4,32,128]{2,1,0:T(8,128)(2,1)S(1)}, bf16[4,32,128]{2,1,0:T(8,128)(2,1)S(1)}, u32[]{:S(2)}, u32[]{:S(2)}) %collective-permute-start.3) | collective-permute-done | bytes 32800 | tf_op jit(solution)/shard_map/ppermute | solution.py:217
  47.4 4.8 %all-to-all-done.main = bf16[64,32,128]{2,1,0:T(8,128)(2,1)S(1)} async-done(((bf16[64,32,128]{2,1,0:T(8,128)(2,1)}), bf16[64,32,128]{2,1,0:T(8,128)(2,1)S(1)}, u32[]{:S(2)}, u32[]{:S(2)}) %all-to-all-start) | async-done | bytes 524320 | tf_op jit(solution)/shard_map/all_to_all | solution.py:212
  52.2 0.0 copy-done.3
  52.2 0.0 copy-done
  52.2 0.0 copy-done.1
  52.2 0.0 copy-done.2
  52.2 2.0 %multiply.1 = (bf16[128,2048]{1,0:T(8,128)(2,1)S(1)}, f32[17,128]{1,0:T(8,128)S(1)}) custom-call(s32[5,32]{1,0:T(8,128)S(1)} %fusion.3.where_at, bf16[64,32,128]{2,1,0:T(8,128)(2,1)S(1)} %all-to-all-done.main, bf16[4,2,32,128]{3,2,1,0:T(8,128)(2,1)S(1)} %copy.13.near, bf16[4,32,128]{2,1,0:T(8,128)(2,1)S(1)} %collective-permute-done.3.above, ...), custom_call_target="tpu_custom_call" | custom-call | tf_op jit(solution)/shard_map/multiply/pallas_call | solution.py:220
  54.3 0.1 broadcast_in_dim.22
  54.4 20.0 %all_to_all.15 = f32[32,17,1,128]{3,2,1,0:T(1,128)S(1)} all-to-all(f32[32,17,1,128]{3,2,1,0:T(1,128)S(1)} %broadcast_in_dim.22), channel_id=1, replica_groups=mesh['y'=4,'c'=2,'z'=16,'x'=4] {'y','c','x'}, dimensions={0} | all-to-all | bytes 557056 | tf_op jit(solution)/shard_map/all_to_all | solution.py:235
  74.4 0.2 reduce_sum.18
  74.5 0.1 broadcast_in_dim.23
  74.6 15.2 %all_to_all.16 = f32[16,17,1,128]{3,2,1,0:T(1,128)S(1)} all-to-all(f32[16,17,1,128]{3,2,1,0:T(1,128)S(1)} %broadcast_in_dim.23), channel_id=1, replica_groups=mesh['y'=4,'c'=2,'z'=16,'x'=4] {'z'}, dimensions={0} | all-to-all | bytes 278528 | tf_op jit(solution)/shard_map/all_to_all | solution.py:235
  89.8 0.1 reduce_sum.19.refs_0_
  89.9 3.0 %finish.1 = (f32[64,2048]{1,0:T(8,128)}, f32[64,64]{1,0:T(8,128)}) custom-call(f32[17,128]{1,0:T(8,128)S(1)} %reduce_sum.19.refs_0_, bf16[128,2048]{1,0:T(8,128)(2,1)S(1)} %get-tuple-element.11.refs_1_), custom_call_target="tpu_custom_call" | custom-call | tf_op jit(solution)/shard_map/finish/pallas_call | solution.py:242
  (5 shorter events, 0.1 us)
Async XLA Ops:
  0.6 51.6 %copy-start.3 = (f32[2048]{0:T(1024)S(1)}, f32[2048]{0:T(1024)}, u32[]{:S(2)}) copy-start(f32[2048]{0:T(1024)} %param.7) | copy-start | bytes 24580
  0.6 41.8 %copy-start.4 = (s32[5,32]{1,0:T(8,128)S(1)}, s32[5,32]{1,0:T(8,128)}, u32[]{:S(2)}) copy-start(s32[5,32]{1,0:T(8,128)} %param.10) | copy-start | bytes 1924
  0.7 51.6 %copy-start = (bf16[5,64,2048]{2,1,0:T(8,128)(2,1)S(1)}, bf16[5,64,2048]{2,1,0:T(8,128)(2,1)}, u32[]{:S(2)}) copy-start(bf16[5,64,2048]{2,1,0:T(8,128)(2,1)} %off.1) | copy-start | bytes 3932164
  0.7 51.6 %copy-start.1 = (bf16[64,2048]{1,0:T(8,128)(2,1)S(1)}, bf16[64,2048]{1,0:T(8,128)(2,1)}, u32[]{:S(2)}) copy-start(bf16[64,2048]{1,0:T(8,128)(2,1)} %diag.1) | copy-start | bytes 786436
  2.9 49.3 %copy-start.2 = (bf16[64,2048]{1,0:T(8,128)(2,1)S(1)}, bf16[64,2048]{1,0:T(8,128)(2,1)}, u32[]{:S(2)}) copy-start(bf16[64,2048]{1,0:T(8,128)(2,1)} %get-tuple-element.9.scaled) | copy-start | bytes 786436
  2.9 49.3 %all-to-all-start = ((bf16[64,32,128]{2,1,0:T(8,128)(2,1)}), bf16[64,32,128]{2,1,0:T(8,128)(2,1)S(1)}, u32[]{:S(2)}, u32[]{:S(2)}) async-start(bf16[64,32,128]{2,1,0:T(8,128)(2,1)} %get-tuple-element.7), calls=%async_computation | async-start | bytes 1048576 | tf_op jit(solution)/shard_map/all_to_all | solution.py:212
  22.9 10.0 %collective-permute-start = (bf16[2,32,128]{2,1,0:T(8,128)(2,1)S(1)}, bf16[2,32,128]{2,1,0:T(8,128)(2,1)S(1)}, u32[]{:S(2)}, u32[]{:S(2)}) collective-permute-start(bf16[2,32,128]{2,1,0:T(8,128)(2,1)S(1)} %get-tuple-element.14), channel_id=1, source_target_pairs={{0,1},{1,0},{2,3},{3,2},{4,5},{5,4},{6,7},{7,6},{8,9},{9,8},{10,11... | collective-permute-start | bytes 49160 | tf_op jit(solution)/shard_map/ppermute | solution.py:213
  25.8 7.1 %collective-permute-start.2 = (bf16[2,32,128]{2,1,0:T(8,128)(2,1)S(1)}, bf16[2,32,128]{2,1,0:T(8,128)(2,1)S(1)}, u32[]{:S(2)}, u32[]{:S(2)}) collective-permute-start(bf16[2,32,128]{2,1,0:T(8,128)(2,1)S(1)} %get-tuple-element.15), channel_id=1, source_target_pairs={{0,3},{1,2},{2,1},{3,0},{4,7},{5,6},{6,5},{7,4},{8,11},{9,10},{10,... | collective-permute-start | bytes 49160 | tf_op jit(solution)/shard_map/ppermute | solution.py:213
  29.5 6.3 %collective-permute-start.1 = (bf16[2,32,128]{2,1,0:T(8,128)(2,1)S(1)}, bf16[2,32,128]{2,1,0:T(8,128)(2,1)S(1)}, u32[]{:S(2)}, u32[]{:S(2)}) collective-permute-start(bf16[2,32,128]{2,1,0:T(8,128)(2,1)S(1)} %get-tuple-element.16), channel_id=1, source_target_pairs={{0,2},{1,3},{2,0},{3,1},{4,6},{5,7},{6,4},{7,5},{8,10},{9,11},{10,... | collective-permute-start | bytes 49160 | tf_op jit(solution)/shard_map/ppermute | solution.py:213
  35.9 7.6 %collective-permute-start.4 = (bf16[4,32,128]{2,1,0:T(8,128)(2,1)S(1)}, bf16[4,32,128]{2,1,0:T(8,128)(2,1)S(1)}, u32[]{:S(2)}, u32[]{:S(2)}) collective-permute-start(bf16[4,32,128]{2,1,0:T(8,128)(2,1)S(1)} %get-tuple-element.12), channel_id=1, source_target_pairs={{4,0},{8,4},{12,8},{16,12},{20,16},{24,20},{28,24},{32,28},{36,32}... | collective-permute-start | bytes 98312 | tf_op jit(solution)/shard_map/ppermute | solution.py:218
  40.5 6.9 %collective-permute-start.3 = (bf16[4,32,128]{2,1,0:T(8,128)(2,1)S(1)}, bf16[4,32,128]{2,1,0:T(8,128)(2,1)S(1)}, u32[]{:S(2)}, u32[]{:S(2)}) collective-permute-start(bf16[4,32,128]{2,1,0:T(8,128)(2,1)S(1)} %get-tuple-element.13), channel_id=1, source_target_pairs={{0,4},{4,8},{8,12},{12,16},{16,20},{20,24},{24,28},{28,32},{32,36}... | collective-permute-start | bytes 98312 | tf_op jit(solution)/shard_map/ppermute | solution.py:217

commit v5 on v4

--- a/solution.py
+++ b/solution.py
@@ -31,7 +31,7 @@
     return lax.broadcasted_iota(jnp.int32, (rows, 128), 1) < 64
 
 
-def pack_kernel(lists_at, panel_at, scale_at, scaled, payload, extra, lists, panel, scale, blocks, sems):
+def pack_kernel(lists_at, panel_at, scale_at, payload, extra, lists, panel, scale, blocks, sems):
     fetches = [
         pltpu.make_async_copy(scale_at, scale, sems.at[0]),
         pltpu.make_async_copy(panel_at, panel, sems.at[1]),
@@ -45,7 +45,6 @@
     for i in range(panel.shape[1] // 128):
         cols = slice(128 * i, 128 * i + 128)
         slab = panel[:, cols].astype(jnp.float32) * scale[i : i + 1, :]
-        scaled[:, cols] = slab.astype(jnp.bfloat16)
         top, low = slab[:32], slab[32:]
         turned = pltpu.roll(slab, 64, 1)
         even = jnp.where(left, top, turned[32:])
@@ -64,7 +63,7 @@
         extra[jnp.bitwise_xor(to, x), 1] = blocks[jnp.maximum(lists[1, second], 0)]
 
 
-def multiply_kernel(where_at, main, near, above, below, scaled, scale, diag, off, halves, gram, table):
+def multiply_kernel(where_at, main, near, above, below, panel, scale, diag, off, halves, gram, table):
     left = left_half(32)
 
     def spread(at, packed):
@@ -82,10 +81,10 @@
         spread(76 + s, below[s])
 
     left64 = left_half(64)
-    for i in range(scaled.shape[1] // 128):
+    for i in range(panel.shape[1] // 128):
         cols = slice(128 * i, 128 * i + 128)
         rows = []
-        own = scaled[:, cols]
+        own = (panel[:, cols].astype(jnp.float32) * scale[i : i + 1, :]).astype(jnp.bfloat16)
         swapped = pltpu.roll(own, 64, 1)
         for b, side in ((2 * i, swapped), (2 * i + 1, own)):
             read = [table[where_at[k, b]] for k in range(5)]
@@ -182,15 +181,14 @@
     panel_width, local_nodes = test_panel.shape
     node_count = local_nodes * NY * NC * NZ * NX
     scale = node_scale.reshape(local_nodes // 128, 128)
-    scaled, payload, extra = pl.pallas_call(
+    payload, extra = pl.pallas_call(
         pack_kernel,
         out_shape=(
-            jax.ShapeDtypeStruct((64, local_nodes), jnp.bfloat16),
             jax.ShapeDtypeStruct((NZ * NX, 32, 128), jnp.bfloat16),
             jax.ShapeDtypeStruct((NX, 2, 32, 128), jnp.bfloat16),
         ),
         in_specs=[outside(), outside(), outside()],
-        out_specs=(vmem(), vmem(), vmem()),
+        out_specs=(vmem(), vmem()),
         scratch_shapes=[
             pltpu.SMEM((2, NZ * NX), jnp.int32),
             pltpu.VMEM((64, local_nodes), jnp.bfloat16),
@@ -228,7 +226,7 @@
         scratch_shapes=[pltpu.VMEM((80, 64, 128), jnp.bfloat16)],
         compiler_params=pltpu.CompilerParams(vmem_limit_bytes=16 * MIB),
         name="multiply",
-    )(where_at, main, near, above, below, scaled, scale, diag_blocks, off_blocks)
+    )(where_at, main, near, above, below, test_panel, scale, diag_blocks, off_blocks)
 
     def summed(part, axes, count):
         copies = jnp.broadcast_to(part[None, :, None], (count, 17, 1, 128))

time: 94.2 us -> 94 us (level)
  no operation moved by 1% of the time
where the time goes in v5:
time: 94 us; the launch traced here: 92.7 us
  blocking collectives  35.2 us (37%)
  starting transfers between devices  34.8 us (37%)
  waiting for transfers between devices  12.6 us (13%)
  Pallas kernels  7.14 us (8%)
  local copies, waits for them, and re-layouts  1.86 us (2%)
    all_to_all x2, blocking collectives, summed(): return lax.all_to_all(copies, axes, 0, 0, tiled=True).sum((0, 2))  35.2 us
    all_to_all x1, starting transfers between devices, shards(): main = lax.all_to_all(payload, ('z', 'x'), 0, 0, tiled=True)  19.1 us
    ppermute x3, starting transfers between devices, shards(): lax.ppermute(extra[d], 'x', [(i, i ^ d) for i in range(NX)])  9.13 us
    all_to_all x1, waiting for transfers between devices, shards(): main = lax.all_to_all(payload, ('z', 'x'), 0, 0, tiled=True)  4.84 us
    ppermute x1, starting transfers between devices, shards(): below = lax.ppermute(near[:, 1], 'z', down)  4.61 us
    ppermute x1, waiting for transfers between devices, shards(): above = lax.ppermute(near[:, 0], 'z', up)  3.87 us
    pallas_call x1, Pallas kernels, shards(): pl.pallas_call(finish, out_shape=(jax.ShapeDtypeStruct((64, local_nodes),...  2.95 us
    ppermute x3, waiting for transfers between devices, shards(): lax.ppermute(extra[d], 'x', [(i, i ^ d) for i in range(NX)])  2.91 us
  transfers between devices with their start and end apart: 6, of which 4 were waited for; matrix products, arithmetic and copies ran while one was open for 2% of the time, Pallas kernels for 0%

profile of v5, /device:TPU:1, one launch (start us, length us, event | category | flops | bytes accessed | tf_op | source)
XLA Modules:
  0.0 92.7 jit_solution(14610955792143951686)
XLA Ops:
  0.6 0.0 copy-start.1
  0.6 0.0 copy-start.3
  0.7 0.0 copy-start.4
  0.7 0.0 copy-start
  0.7 0.0 copy-start.2
  0.7 2.1 %pack.1 = (bf16[64,32,128]{2,1,0:T(8,128)(2,1)}, bf16[4,2,32,128]{3,2,1,0:T(8,128)(2,1)}) custom-call(s32[2,64]{1,0:T(2,128)} %bitcast.20, bf16[64,2048]{1,0:T(8,128)(2,1)} %panel.1, f32[16,128]{1,0:T(8,128)} %bitcast.15), custom_call_target="tpu_custom_call" | custom-call | tf_op jit(solution)/shard_map/pack/pallas_call | solution.py:184
  2.8 19.1 %all-to-all-start = ((bf16[64,32,128]{2,1,0:T(8,128)(2,1)}), bf16[64,32,128]{2,1,0:T(8,128)(2,1)S(1)}, u32[]{:S(2)}, u32[]{:S(2)}) async-start(bf16[64,32,128]{2,1,0:T(8,128)(2,1)} %get-tuple-element.6), calls=%async_computation | async-start | bytes 1048576 | tf_op jit(solution)/shard_map/all_to_all | solution.py:210
  21.9 0.8 slice_bitcast_fusion.4
  22.7 2.9 %collective-permute-start = (bf16[2,32,128]{2,1,0:T(8,128)(2,1)S(1)}, bf16[2,32,128]{2,1,0:T(8,128)(2,1)S(1)}, u32[]{:S(2)}, u32[]{:S(2)}) collective-permute-start(bf16[2,32,128]{2,1,0:T(8,128)(2,1)S(1)} %get-tuple-element.12), channel_id=1, source_target_pairs={{0,1},{1,0},{2,3},{3,2},{4,5},{5,4},{6,7},{7,6},{8,9},{9,8},{10,11... | collective-permute-start | bytes 49160 | tf_op jit(solution)/shard_map/ppermute | solution.py:211
  25.6 3.7 %collective-permute-start.2 = (bf16[2,32,128]{2,1,0:T(8,128)(2,1)S(1)}, bf16[2,32,128]{2,1,0:T(8,128)(2,1)S(1)}, u32[]{:S(2)}, u32[]{:S(2)}) collective-permute-start(bf16[2,32,128]{2,1,0:T(8,128)(2,1)S(1)} %get-tuple-element.13), channel_id=1, source_target_pairs={{0,3},{1,2},{2,1},{3,0},{4,7},{5,6},{6,5},{7,4},{8,11},{9,10},{10,... | collective-permute-start | bytes 49160 | tf_op jit(solution)/shard_map/ppermute | solution.py:211
  29.3 2.5 %collective-permute-start.1 = (bf16[2,32,128]{2,1,0:T(8,128)(2,1)S(1)}, bf16[2,32,128]{2,1,0:T(8,128)(2,1)S(1)}, u32[]{:S(2)}, u32[]{:S(2)}) collective-permute-start(bf16[2,32,128]{2,1,0:T(8,128)(2,1)S(1)} %get-tuple-element.14), channel_id=1, source_target_pairs={{0,2},{1,3},{2,0},{3,1},{4,6},{5,7},{6,4},{7,5},{8,10},{9,11},{10,... | collective-permute-start | bytes 49160 | tf_op jit(solution)/shard_map/ppermute | solution.py:211
  31.9 0.8 copy.12
  32.7 0.0 collective-permute-done
  32.7 0.0 collective-permute-done.2
  32.7 2.9 %collective-permute-done.1 = bf16[2,32,128]{2,1,0:T(8,128)(2,1)S(1)} collective-permute-done((bf16[2,32,128]{2,1,0:T(8,128)(2,1)S(1)}, bf16[2,32,128]{2,1,0:T(8,128)(2,1)S(1)}, u32[]{:S(2)}, u32[]{:S(2)}) %collective-permute-start.1) | collective-permute-done | bytes 16416 | tf_op jit(solution)/shard_map/ppermute | solution.py:211
  35.7 4.6 %collective-permute-start.4 = (bf16[4,32,128]{2,1,0:T(8,128)(2,1)S(1)}, bf16[4,32,128]{2,1,0:T(8,128)(2,1)S(1)}, u32[]{:S(2)}, u32[]{:S(2)}) collective-permute-start(bf16[4,32,128]{2,1,0:T(8,128)(2,1)S(1)} %get-tuple-element.10), channel_id=1, source_target_pairs={{4,0},{8,4},{12,8},{16,12},{20,16},{24,20},{28,24},{32,28},{36,32}... | collective-permute-start | bytes 98312 | tf_op jit(solution)/shard_map/ppermute | solution.py:216
  40.3 1.9 %collective-permute-start.3 = (bf16[4,32,128]{2,1,0:T(8,128)(2,1)S(1)}, bf16[4,32,128]{2,1,0:T(8,128)(2,1)S(1)}, u32[]{:S(2)}, u32[]{:S(2)}) collective-permute-start(bf16[4,32,128]{2,1,0:T(8,128)(2,1)S(1)} %get-tuple-element.11), channel_id=1, source_target_pairs={{0,4},{4,8},{8,12},{12,16},{16,20},{20,24},{24,28},{28,32},{32,36}... | collective-permute-start | bytes 98312 | tf_op jit(solution)/shard_map/ppermute | solution.py:215
  42.2 0.0 copy-done.4
  42.3 1.0 %collective-permute-done.4.below = bf16[4,32,128]{2,1,0:T(8,128)(2,1)S(1)} collective-permute-done((bf16[4,32,128]{2,1,0:T(8,128)(2,1)S(1)}, bf16[4,32,128]{2,1,0:T(8,128)(2,1)S(1)}, u32[]{:S(2)}, u32[]{:S(2)}) %collective-permute-start.4) | collective-permute-done | bytes 32800 | tf_op jit(solution)/shard_map/ppermute | solution.py:216
  43.3 3.9 %collective-permute-done.3.above = bf16[4,32,128]{2,1,0:T(8,128)(2,1)S(1)} collective-permute-done((bf16[4,32,128]{2,1,0:T(8,128)(2,1)S(1)}, bf16[4,32,128]{2,1,0:T(8,128)(2,1)S(1)}, u32[]{:S(2)}, u32[]{:S(2)}) %collective-permute-start.3) | collective-permute-done | bytes 32800 | tf_op jit(solution)/shard_map/ppermute | solution.py:215
  47.1 4.8 %all-to-all-done.main = bf16[64,32,128]{2,1,0:T(8,128)(2,1)S(1)} async-done(((bf16[64,32,128]{2,1,0:T(8,128)(2,1)}), bf16[64,32,128]{2,1,0:T(8,128)(2,1)S(1)}, u32[]{:S(2)}, u32[]{:S(2)}) %all-to-all-start) | async-done | bytes 524320 | tf_op jit(solution)/shard_map/all_to_all | solution.py:210
  52.0 0.0 copy-done.1
  52.0 0.0 copy-done.3
  52.0 0.0 copy-done
  52.0 0.0 copy-done.2
  52.0 2.1 %multiply.1 = (bf16[128,2048]{1,0:T(8,128)(2,1)S(1)}, f32[17,128]{1,0:T(8,128)S(1)}) custom-call(s32[5,32]{1,0:T(8,128)S(1)} %fusion.3.where_at, bf16[64,32,128]{2,1,0:T(8,128)(2,1)S(1)} %all-to-all-done.main, bf16[4,2,32,128]{3,2,1,0:T(8,128)(2,1)S(1)} %copy.13.near, bf16[4,32,128]{2,1,0:T(8,128)(2,1)S(1)} %collective-permute-done.3.above, ...), custom_call_target="tpu_custom_call" | custom-call | tf_op jit(solution)/shard_map/multiply/pallas_call | solution.py:218
  54.1 0.1 broadcast_in_dim.22
  54.2 20.0 %all_to_all.15 = f32[32,17,1,128]{3,2,1,0:T(1,128)S(1)} all-to-all(f32[32,17,1,128]{3,2,1,0:T(1,128)S(1)} %broadcast_in_dim.22), channel_id=1, replica_groups=mesh['y'=4,'c'=2,'z'=16,'x'=4] {'y','c','x'}, dimensions={0} | all-to-all | bytes 557056 | tf_op jit(solution)/shard_map/all_to_all | solution.py:233
  74.2 0.2 reduce_sum.18
  74.4 0.1 broadcast_in_dim.23
  74.4 15.2 %all_to_all.16 = f32[16,17,1,128]{3,2,1,0:T(1,128)S(1)} all-to-all(f32[16,17,1,128]{3,2,1,0:T(1,128)S(1)} %broadcast_in_dim.23), channel_id=1, replica_groups=mesh['y'=4,'c'=2,'z'=16,'x'=4] {'z'}, dimensions={0} | all-to-all | bytes 278528 | tf_op jit(solution)/shard_map/all_to_all | solution.py:233
  89.6 0.1 reduce_sum.19.refs_0_
  89.7 3.0 %finish.1 = (f32[64,2048]{1,0:T(8,128)}, f32[64,64]{1,0:T(8,128)}) custom-call(f32[17,128]{1,0:T(8,128)S(1)} %reduce_sum.19.refs_0_, bf16[128,2048]{1,0:T(8,128)(2,1)S(1)} %get-tuple-element.9.refs_1_), custom_call_target="tpu_custom_call" | custom-call | tf_op jit(solution)/shard_map/finish/pallas_call | solution.py:240
  (5 shorter events, 0.1 us)
Async XLA Ops:
  0.6 51.4 %copy-start.1 = (bf16[64,2048]{1,0:T(8,128)(2,1)S(1)}, bf16[64,2048]{1,0:T(8,128)(2,1)}, u32[]{:S(2)}) copy-start(bf16[64,2048]{1,0:T(8,128)(2,1)} %panel.1) | copy-start | bytes 786436
  0.6 51.4 %copy-start.3 = (f32[2048]{0:T(1024)S(1)}, f32[2048]{0:T(1024)}, u32[]{:S(2)}) copy-start(f32[2048]{0:T(1024)} %param.7) | copy-start | bytes 24580
  0.7 41.6 %copy-start.4 = (s32[5,32]{1,0:T(8,128)S(1)}, s32[5,32]{1,0:T(8,128)}, u32[]{:S(2)}) copy-start(s32[5,32]{1,0:T(8,128)} %param.10) | copy-start | bytes 1924
  0.7 51.3 %copy-start = (bf16[5,64,2048]{2,1,0:T(8,128)(2,1)S(1)}, bf16[5,64,2048]{2,1,0:T(8,128)(2,1)}, u32[]{:S(2)}) copy-start(bf16[5,64,2048]{2,1,0:T(8,128)(2,1)} %off.1) | copy-start | bytes 3932164
  0.7 51.3 %copy-start.2 = (bf16[64,2048]{1,0:T(8,128)(2,1)S(1)}, bf16[64,2048]{1,0:T(8,128)(2,1)}, u32[]{:S(2)}) copy-start(bf16[64,2048]{1,0:T(8,128)(2,1)} %diag.1) | copy-start | bytes 786436
  2.8 49.2 %all-to-all-start = ((bf16[64,32,128]{2,1,0:T(8,128)(2,1)}), bf16[64,32,128]{2,1,0:T(8,128)(2,1)S(1)}, u32[]{:S(2)}, u32[]{:S(2)}) async-start(bf16[64,32,128]{2,1,0:T(8,128)(2,1)} %get-tuple-element.6), calls=%async_computation | async-start | bytes 1048576 | tf_op jit(solution)/shard_map/all_to_all | solution.py:210
  22.7 10.0 %collective-permute-start = (bf16[2,32,128]{2,1,0:T(8,128)(2,1)S(1)}, bf16[2,32,128]{2,1,0:T(8,128)(2,1)S(1)}, u32[]{:S(2)}, u32[]{:S(2)}) collective-permute-start(bf16[2,32,128]{2,1,0:T(8,128)(2,1)S(1)} %get-tuple-element.12), channel_id=1, source_target_pairs={{0,1},{1,0},{2,3},{3,2},{4,5},{5,4},{6,7},{7,6},{8,9},{9,8},{10,11... | collective-permute-start | bytes 49160 | tf_op jit(solution)/shard_map/ppermute | solution.py:211
  25.6 7.1 %collective-permute-start.2 = (bf16[2,32,128]{2,1,0:T(8,128)(2,1)S(1)}, bf16[2,32,128]{2,1,0:T(8,128)(2,1)S(1)}, u32[]{:S(2)}, u32[]{:S(2)}) collective-permute-start(bf16[2,32,128]{2,1,0:T(8,128)(2,1)S(1)} %get-tuple-element.13), channel_id=1, source_target_pairs={{0,3},{1,2},{2,1},{3,0},{4,7},{5,6},{6,5},{7,4},{8,11},{9,10},{10,... | collective-permute-start | bytes 49160 | tf_op jit(solution)/shard_map/ppermute | solution.py:211
  29.3 6.3 %collective-permute-start.1 = (bf16[2,32,128]{2,1,0:T(8,128)(2,1)S(1)}, bf16[2,32,128]{2,1,0:T(8,128)(2,1)S(1)}, u32[]{:S(2)}, u32[]{:S(2)}) collective-permute-start(bf16[2,32,128]{2,1,0:T(8,128)(2,1)S(1)} %get-tuple-element.14), channel_id=1, source_target_pairs={{0,2},{1,3},{2,0},{3,1},{4,6},{5,7},{6,4},{7,5},{8,10},{9,11},{10,... | collective-permute-start | bytes 49160 | tf_op jit(solution)/shard_map/ppermute | solution.py:211
  35.7 7.6 %collective-permute-start.4 = (bf16[4,32,128]{2,1,0:T(8,128)(2,1)S(1)}, bf16[4,32,128]{2,1,0:T(8,128)(2,1)S(1)}, u32[]{:S(2)}, u32[]{:S(2)}) collective-permute-start(bf16[4,32,128]{2,1,0:T(8,128)(2,1)S(1)} %get-tuple-element.10), channel_id=1, source_target_pairs={{4,0},{8,4},{12,8},{16,12},{20,16},{24,20},{28,24},{32,28},{36,32}... | collective-permute-start | bytes 98312 | tf_op jit(solution)/shard_map/ppermute | solution.py:216
  40.3 6.9 %collective-permute-start.3 = (bf16[4,32,128]{2,1,0:T(8,128)(2,1)S(1)}, bf16[4,32,128]{2,1,0:T(8,128)(2,1)S(1)}, u32[]{:S(2)}, u32[]{:S(2)}) collective-permute-start(bf16[4,32,128]{2,1,0:T(8,128)(2,1)S(1)} %get-tuple-element.11), channel_id=1, source_target_pairs={{0,4},{4,8},{8,12},{12,16},{16,20},{20,24},{24,28},{28,32},{32,36}... | collective-permute-start | bytes 98312 | tf_op jit(solution)/shard_map/ppermute | solution.py:215

commit v6 on v5

--- a/solution.py
+++ b/solution.py
@@ -6,6 +6,8 @@
 from jax.sharding import Mesh, PartitionSpec as P
 
 NY, NC, NZ, NX = 4, 2, 16, 4
+NZL = 8
+Z = ("zh", "zl")
 PLANE = ("y", "c", "x")
 NPLANE = NY * NC * NX
 MIB = 1 << 20
@@ -25,6 +27,10 @@
 
 def anywhere():
     return pl.BlockSpec(memory_space=pl.ANY)
+
+
+def place(z, x):
+    return (z // NZL * NX + x) * NZL + z % NZL
 
 
 def left_half(rows):
@@ -45,17 +51,15 @@
     for i in range(panel.shape[1] // 128):
         cols = slice(128 * i, 128 * i + 128)
         slab = panel[:, cols].astype(jnp.float32) * scale[i : i + 1, :]
-        top, low = slab[:32], slab[32:]
+        slab = slab.astype(jnp.bfloat16)
         turned = pltpu.roll(slab, 64, 1)
-        even = jnp.where(left, top, turned[32:])
-        odd = jnp.where(left, turned[:32], low)
-        blocks[2 * i] = even.astype(jnp.bfloat16)
-        blocks[2 * i + 1] = odd.astype(jnp.bfloat16)
-    z, x = lax.axis_index("z"), lax.axis_index("x")
+        blocks[2 * i] = jnp.where(left, slab[:32], turned[32:])
+        blocks[2 * i + 1] = jnp.where(left, turned[:32], slab[32:])
+    z, x = lax.axis_index("zh") * NZL + lax.axis_index("zl"), lax.axis_index("x")
     rank = z * NX + x
     for to in range(NX):
         for zz in range(NZ):
-            payload[zz * NX + to] = blocks[jnp.maximum(lists[0, zz * NX + to], 0)]
+            payload[place(zz, to)] = blocks[jnp.maximum(lists[0, zz * NX + to], 0)]
         step = lax.rem(to - x + NX, NX)
         first = lax.rem(rank + step, NZ * NX)
         second = lax.rem(rank + step - NX + NZ * NX, NZ * NX)
@@ -73,7 +77,7 @@
         table[at, 32:] = jnp.where(left, turned, wide).astype(jnp.bfloat16)
 
     for s in range(NZ * NX):
-        spread(s, main[s])
+        spread(s, main[place(s // NX, s % NX)])
     for s in range(NX):
         spread(64 + s, near[s, 0])
         spread(68 + s, near[s, 1])
@@ -199,7 +203,7 @@
         name="pack",
     )(send_lists.T, test_panel, scale)
 
-    z, x = lax.axis_index("z"), lax.axis_index("x")
+    z, x = lax.axis_index("zh") * NZL + lax.axis_index("zl"), lax.axis_index("x")
     source, entry = block_columns // 2, block_columns % 2
     source_z, source_x = source // NX, source % NX
     apart = source_x ^ x
@@ -207,13 +211,13 @@
     other = jnp.where(source_z == (z + NZ - 1) % NZ, 72, 76) + apart
     where_at = jnp.where(entry == 0, source, jnp.where(source_z == z, same, other))
 
-    main = lax.all_to_all(payload, ("z", "x"), 0, 0, tiled=True)
+    main = lax.all_to_all(payload, ("zh", "x", "zl"), 0, 0, tiled=True)
     moved = [lax.ppermute(extra[d], "x", [(i, i ^ d) for i in range(NX)]) for d in (1, 2, 3)]
     near = jnp.stack([extra[0]] + moved)
     up = [(i, (i + 1) % NZ) for i in range(NZ)]
     down = [((i + 1) % NZ, i) for i in range(NZ)]
-    above = lax.ppermute(near[:, 0], "z", up)
-    below = lax.ppermute(near[:, 1], "z", down)
+    above = lax.ppermute(near[:, 0], Z, up)
+    below = lax.ppermute(near[:, 1], Z, down)
 
     halves, gram = pl.pallas_call(
         multiply_kernel,
@@ -232,7 +236,7 @@
         copies = jnp.broadcast_to(part[None, :, None], (count, 17, 1, 128))
         return lax.all_to_all(copies, axes, 0, 0, tiled=True).sum((0, 2))
 
-    gram = summed(summed(gram, PLANE, NPLANE), "z", NZ)
+    gram = summed(summed(gram, PLANE, NPLANE), Z, NZ)
 
     def finish(*refs):
         finish_kernel(node_count, *refs)
@@ -256,8 +260,8 @@
 
 
 def solution(mesh):
-    split = Mesh(mesh.devices.reshape(NY, NC, NZ, NX), ("y", "c", "z", "x"))
-    every = ("y", "c", "z", "x")
+    split = Mesh(mesh.devices.reshape(NY, NC, NZ // NZL, NZL, NX), ("y", "c", "zh", "zl", "x"))
+    every = ("y", "c", "zh", "zl", "x")
     in_specs = (
         P(None, every),
         P(every),

time: 94 us -> 94 us (level)
  waiting for transfers between devices: 12.6 us -> 11.2 us
  blocking collectives: 35.2 us -> 36.6 us
    all_to_all x2, blocking collectives: 35.2 us -> 36.6 us  [summed(): return lax.all_to_all(copies, axes, 0, 0, tiled=True).sum((0, 2))]
    all_to_all x1, waiting for transfers between devices: 4.84 us -> 3.48 us  [shards(): main = lax.all_to_all(payload, ('zh', 'x', 'zl'), 0, 0, tiled=True)]
where the time goes in v6:
time: 94 us; the launch traced here: 92.7 us
  blocking collectives  36.6 us (39%)
  starting transfers between devices  34.8 us (37%)
  waiting for transfers between devices  11.2 us (12%)
  Pallas kernels  7.13 us (8%)
  local copies, waits for them, and re-layouts  1.86 us (2%)
    all_to_all x2, blocking collectives, summed(): return lax.all_to_all(copies, axes, 0, 0, tiled=True).sum((0, 2))  36.6 us
    all_to_all x1, starting transfers between devices, shards(): main = lax.all_to_all(payload, ('zh', 'x', 'zl'), 0, 0, tiled=True)  19.1 us
    ppermute x3, starting transfers between devices, shards(): lax.ppermute(extra[d], 'x', [(i, i ^ d) for i in range(NX)])  9.17 us
    ppermute x1, starting transfers between devices, shards(): below = lax.ppermute(near[:, 1], Z, down)  4.57 us
    ppermute x1, waiting for transfers between devices, shards(): above = lax.ppermute(near[:, 0], Z, up)  3.87 us
    all_to_all x1, waiting for transfers between devices, shards(): main = lax.all_to_all(payload, ('zh', 'x', 'zl'), 0, 0, tiled=True)  3.48 us
    pallas_call x1, Pallas kernels, shards(): pl.pallas_call(finish, out_shape=(jax.ShapeDtypeStruct((64, local_nodes),...  2.95 us
    ppermute x3, waiting for transfers between devices, shards(): lax.ppermute(extra[d], 'x', [(i, i ^ d) for i in range(NX)])  2.85 us
  transfers between devices with their start and end apart: 6, of which 4 were waited for; matrix products, arithmetic and copies ran while one was open for 2% of the time, Pallas kernels for 0%

profile of v6, /device:TPU:1, one launch (start us, length us, event | category | flops | bytes accessed | tf_op | source)
XLA Modules:
  0.0 92.7 jit_solution(11669021844622437414)
XLA Ops:
  0.6 0.0 copy-start.1
  0.6 0.0 copy-start.3
  0.7 0.0 copy-start.4
  0.7 0.0 copy-start
  0.7 0.0 copy-start.2
  0.7 2.1 %pack.1 = (bf16[64,32,128]{2,1,0:T(8,128)(2,1)}, bf16[4,2,32,128]{3,2,1,0:T(8,128)(2,1)}) custom-call(s32[2,64]{1,0:T(2,128)} %bitcast.20, bf16[64,2048]{1,0:T(8,128)(2,1)} %panel.1, f32[16,128]{1,0:T(8,128)} %bitcast.15), custom_call_target="tpu_custom_call" | custom-call | tf_op jit(solution)/shard_map/pack/pallas_call | solution.py:188
  2.8 19.1 %all-to-all-start = ((bf16[64,32,128]{2,1,0:T(8,128)(2,1)}), bf16[64,32,128]{2,1,0:T(8,128)(2,1)S(1)}, u32[]{:S(2)}, u32[]{:S(2)}) async-start(bf16[64,32,128]{2,1,0:T(8,128)(2,1)} %get-tuple-element.6), calls=%async_computation | async-start | bytes 1048576 | tf_op jit(solution)/shard_map/all_to_all | solution.py:214
  21.9 0.8 slice_bitcast_fusion.4
  22.7 2.9 %collective-permute-start = (bf16[2,32,128]{2,1,0:T(8,128)(2,1)S(1)}, bf16[2,32,128]{2,1,0:T(8,128)(2,1)S(1)}, u32[]{:S(2)}, u32[]{:S(2)}) collective-permute-start(bf16[2,32,128]{2,1,0:T(8,128)(2,1)S(1)} %get-tuple-element.12), channel_id=1, source_target_pairs={{0,1},{1,0},{2,3},{3,2},{4,5},{5,4},{6,7},{7,6},{8,9},{9,8},{10,11... | collective-permute-start | bytes 49160 | tf_op jit(solution)/shard_map/ppermute | solution.py:215
  25.6 3.7 %collective-permute-start.2 = (bf16[2,32,128]{2,1,0:T(8,128)(2,1)S(1)}, bf16[2,32,128]{2,1,0:T(8,128)(2,1)S(1)}, u32[]{:S(2)}, u32[]{:S(2)}) collective-permute-start(bf16[2,32,128]{2,1,0:T(8,128)(2,1)S(1)} %get-tuple-element.13), channel_id=1, source_target_pairs={{0,3},{1,2},{2,1},{3,0},{4,7},{5,6},{6,5},{7,4},{8,11},{9,10},{10,... | collective-permute-start | bytes 49160 | tf_op jit(solution)/shard_map/ppermute | solution.py:215
  29.3 2.6 %collective-permute-start.1 = (bf16[2,32,128]{2,1,0:T(8,128)(2,1)S(1)}, bf16[2,32,128]{2,1,0:T(8,128)(2,1)S(1)}, u32[]{:S(2)}, u32[]{:S(2)}) collective-permute-start(bf16[2,32,128]{2,1,0:T(8,128)(2,1)S(1)} %get-tuple-element.14), channel_id=1, source_target_pairs={{0,2},{1,3},{2,0},{3,1},{4,6},{5,7},{6,4},{7,5},{8,10},{9,11},{10,... | collective-permute-start | bytes 49160 | tf_op jit(solution)/shard_map/ppermute | solution.py:215
  31.9 0.8 copy.12
  32.8 0.0 collective-permute-done
  32.8 0.0 collective-permute-done.2
  32.8 2.8 %collective-permute-done.1 = bf16[2,32,128]{2,1,0:T(8,128)(2,1)S(1)} collective-permute-done((bf16[2,32,128]{2,1,0:T(8,128)(2,1)S(1)}, bf16[2,32,128]{2,1,0:T(8,128)(2,1)S(1)}, u32[]{:S(2)}, u32[]{:S(2)}) %collective-permute-start.1) | collective-permute-done | bytes 16416 | tf_op jit(solution)/shard_map/ppermute | solution.py:215
  35.6 4.6 %collective-permute-start.4 = (bf16[4,32,128]{2,1,0:T(8,128)(2,1)S(1)}, bf16[4,32,128]{2,1,0:T(8,128)(2,1)S(1)}, u32[]{:S(2)}, u32[]{:S(2)}) collective-permute-start(bf16[4,32,128]{2,1,0:T(8,128)(2,1)S(1)} %get-tuple-element.10), channel_id=1, source_target_pairs={{4,0},{8,4},{12,8},{16,12},{20,16},{24,20},{28,24},{32,28},{36,32}... | collective-permute-start | bytes 98312 | tf_op jit(solution)/shard_map/ppermute | solution.py:220
  40.2 1.9 %collective-permute-start.3 = (bf16[4,32,128]{2,1,0:T(8,128)(2,1)S(1)}, bf16[4,32,128]{2,1,0:T(8,128)(2,1)S(1)}, u32[]{:S(2)}, u32[]{:S(2)}) collective-permute-start(bf16[4,32,128]{2,1,0:T(8,128)(2,1)S(1)} %get-tuple-element.11), channel_id=1, source_target_pairs={{0,4},{4,8},{8,12},{12,16},{16,20},{20,24},{24,28},{28,32},{32,36}... | collective-permute-start | bytes 98312 | tf_op jit(solution)/shard_map/ppermute | solution.py:219
  42.2 0.0 copy-done.4
  42.2 1.0 %collective-permute-done.4.below = bf16[4,32,128]{2,1,0:T(8,128)(2,1)S(1)} collective-permute-done((bf16[4,32,128]{2,1,0:T(8,128)(2,1)S(1)}, bf16[4,32,128]{2,1,0:T(8,128)(2,1)S(1)}, u32[]{:S(2)}, u32[]{:S(2)}) %collective-permute-start.4) | collective-permute-done | bytes 32800 | tf_op jit(solution)/shard_map/ppermute | solution.py:220
  43.2 3.9 %collective-permute-done.3.above = bf16[4,32,128]{2,1,0:T(8,128)(2,1)S(1)} collective-permute-done((bf16[4,32,128]{2,1,0:T(8,128)(2,1)S(1)}, bf16[4,32,128]{2,1,0:T(8,128)(2,1)S(1)}, u32[]{:S(2)}, u32[]{:S(2)}) %collective-permute-start.3) | collective-permute-done | bytes 32800 | tf_op jit(solution)/shard_map/ppermute | solution.py:219
  47.0 3.5 %all-to-all-done.main = bf16[64,32,128]{2,1,0:T(8,128)(2,1)S(1)} async-done(((bf16[64,32,128]{2,1,0:T(8,128)(2,1)}), bf16[64,32,128]{2,1,0:T(8,128)(2,1)S(1)}, u32[]{:S(2)}, u32[]{:S(2)}) %all-to-all-start) | async-done | bytes 524320 | tf_op jit(solution)/shard_map/all_to_all | solution.py:214
  50.5 0.0 copy-done.1
  50.5 0.0 copy-done.3
  50.5 0.0 copy-done
  50.5 0.0 copy-done.2
  50.6 2.1 %multiply.1 = (bf16[128,2048]{1,0:T(8,128)(2,1)S(1)}, f32[17,128]{1,0:T(8,128)S(1)}) custom-call(s32[5,32]{1,0:T(8,128)S(1)} %fusion.3.where_at, bf16[64,32,128]{2,1,0:T(8,128)(2,1)S(1)} %all-to-all-done.main, bf16[4,2,32,128]{3,2,1,0:T(8,128)(2,1)S(1)} %copy.13.near, bf16[4,32,128]{2,1,0:T(8,128)(2,1)S(1)} %collective-permute-done.3.above, ...), custom_call_target="tpu_custom_call" | custom-call | tf_op jit(solution)/shard_map/multiply/pallas_call | solution.py:222
  52.6 0.1 broadcast_in_dim.22
  52.8 21.4 %all_to_all.15 = f32[32,17,1,128]{3,2,1,0:T(1,128)S(1)} all-to-all(f32[32,17,1,128]{3,2,1,0:T(1,128)S(1)} %broadcast_in_dim.22), channel_id=1, replica_groups=mesh['y'=4,'c'=2,'zh'=2,'zl'=8,'x'=4] {'y','c','x'}, dimensions={0} | all-to-all | bytes 557056 | tf_op jit(solution)/shard_map/all_to_all | solution.py:237
  74.2 0.2 reduce_sum.18
  74.4 0.1 broadcast_in_dim.23
  74.4 15.2 %all_to_all.16 = f32[16,17,1,128]{3,2,1,0:T(1,128)S(1)} all-to-all(f32[16,17,1,128]{3,2,1,0:T(1,128)S(1)} %broadcast_in_dim.23), channel_id=1, replica_groups=mesh['y'=4,'c'=2,'zh'=2,'zl'=8,'x'=4] {'zh','zl'}, dimensions={0} | all-to-all | bytes 278528 | tf_op jit(solution)/shard_map/all_to_all | solution.py:237
  89.6 0.1 reduce_sum.19.refs_0_
  89.7 3.0 %finish.1 = (f32[64,2048]{1,0:T(8,128)}, f32[64,64]{1,0:T(8,128)}) custom-call(f32[17,128]{1,0:T(8,128)S(1)} %reduce_sum.19.refs_0_, bf16[128,2048]{1,0:T(8,128)(2,1)S(1)} %get-tuple-element.9.refs_1_), custom_call_target="tpu_custom_call" | custom-call | tf_op jit(solution)/shard_map/finish/pallas_call | solution.py:244
  (5 shorter events, 0.1 us)
Async XLA Ops:
  0.6 49.9 %copy-start.1 = (bf16[64,2048]{1,0:T(8,128)(2,1)S(1)}, bf16[64,2048]{1,0:T(8,128)(2,1)}, u32[]{:S(2)}) copy-start(bf16[64,2048]{1,0:T(8,128)(2,1)} %panel.1) | copy-start | bytes 786436
  0.6 49.9 %copy-start.3 = (f32[2048]{0:T(1024)S(1)}, f32[2048]{0:T(1024)}, u32[]{:S(2)}) copy-start(f32[2048]{0:T(1024)} %param.7) | copy-start | bytes 24580
  0.7 41.5 %copy-start.4 = (s32[5,32]{1,0:T(8,128)S(1)}, s32[5,32]{1,0:T(8,128)}, u32[]{:S(2)}) copy-start(s32[5,32]{1,0:T(8,128)} %param.10) | copy-start | bytes 1924
  0.7 49.9 %copy-start = (bf16[5,64,2048]{2,1,0:T(8,128)(2,1)S(1)}, bf16[5,64,2048]{2,1,0:T(8,128)(2,1)}, u32[]{:S(2)}) copy-start(bf16[5,64,2048]{2,1,0:T(8,128)(2,1)} %off.1) | copy-start | bytes 3932164
  0.7 49.9 %copy-start.2 = (bf16[64,2048]{1,0:T(8,128)(2,1)S(1)}, bf16[64,2048]{1,0:T(8,128)(2,1)}, u32[]{:S(2)}) copy-start(bf16[64,2048]{1,0:T(8,128)(2,1)} %diag.1) | copy-start | bytes 786436
  2.8 47.7 %all-to-all-start = ((bf16[64,32,128]{2,1,0:T(8,128)(2,1)}), bf16[64,32,128]{2,1,0:T(8,128)(2,1)S(1)}, u32[]{:S(2)}, u32[]{:S(2)}) async-start(bf16[64,32,128]{2,1,0:T(8,128)(2,1)} %get-tuple-element.6), calls=%async_computation | async-start | bytes 1048576 | tf_op jit(solution)/shard_map/all_to_all | solution.py:214
  22.7 10.1 %collective-permute-start = (bf16[2,32,128]{2,1,0:T(8,128)(2,1)S(1)}, bf16[2,32,128]{2,1,0:T(8,128)(2,1)S(1)}, u32[]{:S(2)}, u32[]{:S(2)}) collective-permute-start(bf16[2,32,128]{2,1,0:T(8,128)(2,1)S(1)} %get-tuple-element.12), channel_id=1, source_target_pairs={{0,1},{1,0},{2,3},{3,2},{4,5},{5,4},{6,7},{7,6},{8,9},{9,8},{10,11... | collective-permute-start | bytes 49160 | tf_op jit(solution)/shard_map/ppermute | solution.py:215
  25.6 7.2 %collective-permute-start.2 = (bf16[2,32,128]{2,1,0:T(8,128)(2,1)S(1)}, bf16[2,32,128]{2,1,0:T(8,128)(2,1)S(1)}, u32[]{:S(2)}, u32[]{:S(2)}) collective-permute-start(bf16[2,32,128]{2,1,0:T(8,128)(2,1)S(1)} %get-tuple-element.13), channel_id=1, source_target_pairs={{0,3},{1,2},{2,1},{3,0},{4,7},{5,6},{6,5},{7,4},{8,11},{9,10},{10,... | collective-permute-start | bytes 49160 | tf_op jit(solution)/shard_map/ppermute | solution.py:215
  29.3 6.3 %collective-permute-start.1 = (bf16[2,32,128]{2,1,0:T(8,128)(2,1)S(1)}, bf16[2,32,128]{2,1,0:T(8,128)(2,1)S(1)}, u32[]{:S(2)}, u32[]{:S(2)}) collective-permute-start(bf16[2,32,128]{2,1,0:T(8,128)(2,1)S(1)} %get-tuple-element.14), channel_id=1, source_target_pairs={{0,2},{1,3},{2,0},{3,1},{4,6},{5,7},{6,4},{7,5},{8,10},{9,11},{10,... | collective-permute-start | bytes 49160 | tf_op jit(solution)/shard_map/ppermute | solution.py:215
  35.6 7.5 %collective-permute-start.4 = (bf16[4,32,128]{2,1,0:T(8,128)(2,1)S(1)}, bf16[4,32,128]{2,1,0:T(8,128)(2,1)S(1)}, u32[]{:S(2)}, u32[]{:S(2)}) collective-permute-start(bf16[4,32,128]{2,1,0:T(8,128)(2,1)S(1)} %get-tuple-element.10), channel_id=1, source_target_pairs={{4,0},{8,4},{12,8},{16,12},{20,16},{24,20},{28,24},{32,28},{36,32}... | collective-permute-start | bytes 98312 | tf_op jit(solution)/shard_map/ppermute | solution.py:220
  40.2 6.8 %collective-permute-start.3 = (bf16[4,32,128]{2,1,0:T(8,128)(2,1)S(1)}, bf16[4,32,128]{2,1,0:T(8,128)(2,1)S(1)}, u32[]{:S(2)}, u32[]{:S(2)}) collective-permute-start(bf16[4,32,128]{2,1,0:T(8,128)(2,1)S(1)} %get-tuple-element.11), channel_id=1, source_target_pairs={{0,4},{4,8},{8,12},{12,16},{16,20},{20,24},{24,28},{28,32},{32,36}... | collective-permute-start | bytes 98312 | tf_op jit(solution)/shard_map/ppermute | solution.py:219
